TPU v7x, 128 devices: a whole 4x4x4 slice. The times are simulated.
128 devices in a mesh: dp: 8 (over x_lo, z), cell: 16 (over x_hi, y, core).
Axes of the slice: x: 4 (x_hi: 2, x_lo: 2; x = x_hi * 2 + x_lo), y: 4, z: 4, core: 2. Of those that a mesh axis runs over, the one named last changes fastest.
Arguments:
- sensitivity: float32 [4096, 65536], P(('dp', 'cell')), may hold values from -0.09375 to 0.09375
- row_period: int32 [4096], P(('dp', 'cell')), may hold values from 0 to 31
- row_site: int32 [4096], P(('dp', 'cell')), may hold values from 0 to 127
- period_err: float32 [32], replicated, may hold values from 0.2 to 2
- site_err: float32 [128], replicated, may hold values from 0.2 to 2
- cell_var: float32 [65536], replicated, may hold values from 0.25 to 4
- cell_perm: int32 [65536], replicated, may hold values from 0 to 65535, each once
Outputs:
- gram: float32 [4096, 4096], P('cell', 'dp')
Inputs may be any that keep to these rules, and one draw needn't show every extreme that they name: `cell_perm`: a permutation of 0 to 65535.
All inputs are finite; a program needn't handle non-finite values.
Results may differ from a plain program's by a relative error of at most 0.0009.
Values may be sent and summed in bfloat16 or wider, within the bound.
No kernel may reach another device: no remote copies, remote signals or barrier semaphores. Data moves between devices by JAX's collectives and lax.ppermute only.
A program may use at most 128 MiB of HBM per device.

v0:
```python
import functools

import jax
import jax.numpy as jnp
from jax import lax
from jax.experimental import pallas as pl
from jax.experimental.pallas import tpu as pltpu
from jax.sharding import Mesh, PartitionSpec as P


AXES = ("xl", "z", "xh", "y", "core")
SIZES = (2, 4, 2, 4, 2)
PLANE = ("z", "y", "core")
RING = ("xl", "xh", "core")
CHUNKS = 2
INTERPRET = False


def row_weights(row_period, row_site, period_err, site_err):
    period_hit = row_period[:, None] == jnp.arange(period_err.shape[0], dtype=jnp.int32)[None, :]
    site_hit = row_site[:, None] == jnp.arange(site_err.shape[0], dtype=jnp.int32)[None, :]
    period_scale = jnp.sum(jnp.where(period_hit, period_err[None, :], 0.0), axis=1)
    site_scale = jnp.sum(jnp.where(site_hit, site_err[None, :], 0.0), axis=1)
    return 1.0 / jnp.sqrt(period_scale * period_scale + site_scale * site_scale)


def flat(xl, z, xh, y, core):
    return (((xl * 4 + z) * 2 + xh) * 4 + y) * 2 + core


def ring_index(x, core):
    return ((x % 2) * 2 + x // 2) * 2 + core


def to_ring_neighbour():
    pairs = []
    for x in range(4):
        pairs.append((ring_index((x + 1) % 4, 0), ring_index(x, 0)))
        pairs.append((ring_index((x - 1) % 4, 1), ring_index(x, 1)))
    return pairs


def plane_shift(shift, first):
    pairs = []
    for z in range(4):
        for y in range(4):
            for core in range(2):
                along_y = (core == 0) == first
                to_z, to_y = (z, (y + shift) % 4) if along_y else ((z + shift) % 4, y)
                pairs.append(((z * 4 + y) * 2 + core, (to_z * 4 + to_y) * 2 + core))
    return pairs


def homes(place):
    pairs = []
    for xl in range(2):
        for z in range(4):
            for xh in range(2):
                for y in range(4):
                    for core in range(2):
                        source = place(xl, z, xh, y, core)
                        if source is not None:
                            pairs.append((flat(*source), flat(xl, z, xh, y, core)))
    return pairs


def near_source(half, mirrored):
    def place(xl, z, xh, y, core):
        if xh == xl:
            return None
        forward = (2 * core + xh - (2 * half + xl)) % 4 == 1
        holder = 0 if forward else 1
        if mirrored:
            return (xh, y, core, z, 1 - holder)
        return (xl, z, half, y, holder)

    return place


def own_source(part):
    return lambda xl, z, xh, y, core: (xl, z, core, y, part) if xh == xl else None


def far_source(part, mirrored):
    def place(xl, z, xh, y, core):
        if xh != xl:
            return None
        return (xl, y, core, z, part) if mirrored else (xl, z, 1 - core, y, part)

    return place


def tile_kernel(scal_ref, *refs, chunks, n_out):
    lhs, rhs = refs[:chunks], refs[chunks : 2 * chunks]
    outs, scratch = refs[2 * chunks : 2 * chunks + n_out], refs[-1]
    c = pl.program_id(0)
    height, _ = scratch.shape[2:]
    total = None
    for a, b in zip(lhs, rhs):
        part = lax.dot_general(
            a[...].reshape(4 * height, a.shape[-1]),
            b[...],
            (((1,), (1,)), ((), ())),
            preferred_element_type=jnp.float32,
        )
        total = part if total is None else total + part
    across = lax.rem(c + 4 - scal_ref[1], 4)
    for r in range(4):
        down = lax.rem(r + 4 - scal_ref[0], 4)
        s = jnp.where(scal_ref[2] == 0, down, across)
        v = jnp.where(scal_ref[2] == 0, across, down)
        scratch[s, v] = total[r * height : (r + 1) * height]

    @pl.when(c == 3)
    def _():
        if n_out == 1:
            outs[0][...] = scratch[...]
        else:
            for i in range(4):
                outs[i][...] = scratch[i]


def tile_products(lhs, rhs, scalars, split, joined, windowed):
    rows, depth = lhs[0].shape
    tile = rows // 4
    height = tile // 2 if split else tile
    chunks = len(lhs)
    lhs = [a.reshape(4, tile // height, height, depth) for a in lhs]
    if joined:
        out_shape = [jax.ShapeDtypeStruct((4, 4, height, tile), jnp.float32)]
        out_specs = [pl.BlockSpec((4, 4, height, tile), lambda c, scal: (0, 0, 0, 0))]
    else:
        out_shape = [jax.ShapeDtypeStruct((4, height, tile), jnp.float32)] * 4
        out_specs = [pl.BlockSpec((4, height, tile), lambda c, scal: (0, 0, 0))] * 4
    return pl.pallas_call(
        functools.partial(tile_kernel, chunks=chunks, n_out=len(out_shape)),
        out_shape=out_shape,
        grid_spec=pltpu.PrefetchScalarGridSpec(
            num_scalar_prefetch=1,
            grid=(4,),
            in_specs=[
                pl.BlockSpec(
                    (4, 1, height, depth),
                    lambda c, scal: (0, scal[3], 0, 0),
                    pipeline_mode=pl.Buffered(1),
                )
            ]
            * chunks
            + [pl.BlockSpec((tile, depth), lambda c, scal: (c, scal[4] if windowed else 0))] * chunks,
            out_specs=out_specs,
            scratch_shapes=[pltpu.VMEM((4, 4, height, tile), jnp.float32)],
        ),
        compiler_params=pltpu.CompilerParams(dimension_semantics=("arbitrary",), vmem_limit_bytes=(14 if split else 24) * 2**20),
        cost_estimate=pl.CostEstimate(
            flops=2 * 16 * height * tile * depth * chunks,
            bytes_accessed=16 * height * tile * 4 + chunks * (height * 4 + rows) * depth * 2,
            transcendentals=0,
        ),
        interpret=INTERPRET,
    )(scalars, *lhs, *rhs)


def reduce_plane(strips):
    total = strips[0]
    for shift in (1, 3, 2):
        total = total + lax.ppermute(strips[shift], PLANE, plane_shift(shift, True))
    tile = total[0]
    for shift in (1, 3, 2):
        tile = tile + lax.ppermute(total[shift], PLANE, plane_shift(shift, False))
    return tile


def swap_cores(value):
    return lax.ppermute(value, "core", [(0, 1), (1, 0)])


def finish_kernel(scal_ref, *refs):
    near, own, far, out = refs[:4], refs[4:6], refs[6:10], refs[10]
    height, tile = own[0].shape

    @pl.when(scal_ref[0] == 0)
    def _():
        for half in range(2):
            out[:, half * tile : (half + 1) * tile] = near[2 * half][...] + near[2 * half + 1][...].T

    for half in range(2):

        @pl.when((scal_ref[0] == 1) & (scal_ref[1] == half))
        def _(half=half):
            other = (1 - half) * tile
            for part in range(2):
                rows = slice(part * height, (part + 1) * height)
                out[rows, half * tile : (half + 1) * tile] = own[part][...]
                mirrored = jnp.concatenate(
                    [far[2 + piece][:, rows].T for piece in range(2)], axis=1
                )
                out[rows, other : other + tile] = far[part][...] + mirrored


def finish(scalars, near, own, far):
    _, tile = own[0].shape
    operands = [*near, *own, *far]
    return pl.pallas_call(
        finish_kernel,
        out_shape=jax.ShapeDtypeStruct((tile, 2 * tile), jnp.float32),
        in_specs=[pl.BlockSpec(memory_space=pltpu.SMEM)]
        + [pl.BlockSpec(memory_space=pltpu.VMEM)] * len(operands),
        out_specs=pl.BlockSpec(memory_space=pltpu.VMEM),
        cost_estimate=pl.CostEstimate(
            flops=tile * tile * 2, bytes_accessed=tile * tile * 4 * 9, transcendentals=0
        ),
        interpret=INTERPRET,
    )(scalars, *operands)


def body(sensitivity, row_period, row_site, period_err, site_err, cell_var, cell_perm):
    xl, z, xh, y, core = (lax.axis_index(name).astype(jnp.int32) for name in AXES)
    x = 2 * xh + xl
    cells = cell_var.shape[0]
    chunk = cells // CHUNKS
    depth = chunk // 32
    weight = row_weights(row_period, row_site, period_err, site_err)[:, None]

    first = ((z * 4 + y) * 2 + core) * depth
    positions = jnp.concatenate([lax.dynamic_slice_in_dim(cell_perm, j * chunk + first, depth) for j in range(CHUNKS)])
    column_var = cell_var[positions]

    scaled = []
    for j in range(CHUNKS):
        packed = (weight * sensitivity[:, j * chunk : (j + 1) * chunk]).astype(jnp.bfloat16)
        if j + 1 < CHUNKS:
            weight, packed = lax.optimization_barrier((weight, packed))
        scaled.append(lax.all_to_all(packed, PLANE, split_axis=1, concat_axis=0, tiled=True))

    window = x // 2
    target = lax.rem(x + jnp.where(core == 0, 3, 1), 4)
    weighted, near, far = [], [], []
    for j in range(CHUNKS):
        near.append(lax.ppermute(scaled[j], RING, to_ring_neighbour()))
        var = column_var[None, j * depth : (j + 1) * depth]
        weighted.append((scaled[j].astype(jnp.float32) * var).astype(jnp.bfloat16))
        cut = lax.dynamic_slice_in_dim(near[j], (target // 2) * (depth // 2), depth // 2, 1)
        far.append(lax.ppermute(cut, RING, to_ring_neighbour()))

    def scalars(order, half):
        return jnp.stack([y, z, order, half, window]).astype(jnp.int32)

    def halves(lhs, windowed):
        sent = tile_products(lhs, weighted, scalars(1 - core, 1 - core), True, True, windowed)[0]
        got = swap_cores(sent)
        kept = tile_products(lhs, weighted, scalars(core, core), True, False, windowed)
        strips = [kept[s] + got[s] for s in range(4)]
        return reduce_plane(strips)

    own_tile = halves(scaled, False)
    strips = tile_products(near, weighted, scalars(core, 0 * core), False, False, False)
    near_tile = reduce_plane(strips)
    far_tile = halves(far, True)

    def fetch(value, place):
        return lax.ppermute(value, AXES, homes(place))

    own = [fetch(own_tile, own_source(part)) for part in (0, 1)]
    pair = [fetch(near_tile, near_source(half, mirrored)) for half in (0, 1) for mirrored in (False, True)]
    two = [fetch(far_tile, far_source(part, mirrored)) for mirrored in (False, True) for part in (0, 1)]
    return finish(jnp.stack([(xh == xl).astype(jnp.int32), core]), pair, own, two)


def solution(mesh):
    fine = Mesh(mesh.devices.reshape(SIZES), AXES)

    return jax.shard_map(
        body,
        mesh=fine,
        in_specs=(P(AXES, None), P(AXES), P(AXES), P(), P(), P(), P()),
        out_specs=P(("xh", "y", "core"), ("xl", "z")),
        check_vma=False,
    )
```

profile of v0, /device:TPU:31, one launch (start us, length us, event | category | flops | bytes accessed | tf_op | source)
XLA Modules:
  0.0 267.8 jit_solution(2086367955791207442)
XLA Ops:
  1.8 2.5 multiply_convert_fusion.3
  4.3 2.5 multiply_convert_fusion.2
  8.4 8.7 %all-to-all-start.1 = ((bf16[32,32,1024]{2,0,1:T(8,128)(2,1)}), bf16[32,32,1024]{2,0,1:T(8,128)(2,1)}, u32[]{:S(2)}, u32[]{:S(2)}) async-start(bf16[32,32,1024]{2,0,1:T(8,128)(2,1)} %bitcast.130), calls=%async_computation.1 | async-start | bytes 4194304 | tf_op jit(solution)/shard_map/all_to_all | solution.py:233
  18.6 26.0 %all-to-all-done.1 = bf16[32,32,1024]{2,0,1:T(8,128)(2,1)} async-done(((bf16[32,32,1024]{2,0,1:T(8,128)(2,1)}), bf16[32,32,1024]{2,0,1:T(8,128)(2,1)}, u32[]{:S(2)}, u32[]{:S(2)}) %all-to-all-start.1) | async-done | bytes 2097184 | tf_op jit(solution)/shard_map/all_to_all | solution.py:233
  44.7 7.1 %all-to-all-start = ((bf16[32,32,1024]{2,0,1:T(8,128)(2,1)}), bf16[32,32,1024]{2,0,1:T(8,128)(2,1)}, u32[]{:S(2)}, u32[]{:S(2)}) async-start(bf16[32,32,1024]{2,0,1:T(8,128)(2,1)} %bitcast.129), calls=%async_computation | async-start | bytes 4194304 | tf_op jit(solution)/shard_map/all_to_all | solution.py:233
  52.5 11.8 %gather_fusion = f32[2048]{0:T(1024)S(1)} fusion(f32[65536]{0:T(1024)S(1)} %copy-done, s32[2048]{0:T(1024)S(1)} %broadcast_clamp_fusion), kind=kCustom, calls=%fused_computation | custom fusion | bytes 24576 | tf_op jit(solution)/shard_map/gather | solution.py:226
  64.6 14.9 %all-to-all-done = bf16[32,32,1024]{2,0,1:T(8,128)(2,1)} async-done(((bf16[32,32,1024]{2,0,1:T(8,128)(2,1)}), bf16[32,32,1024]{2,0,1:T(8,128)(2,1)}, u32[]{:S(2)}, u32[]{:S(2)}) %all-to-all-start) | async-done | bytes 2097184 | tf_op jit(solution)/shard_map/all_to_all | solution.py:233
  79.8 2.2 multiply_convert_fusion.1.refs_2_
  81.9 2.1 multiply_convert_fusion.refs_3_
  84.1 6.8 %shard_map.75 = f32[4,4,128,256]{3,2,1,0:T(8,128)} custom-call(s32[5]{0:T(128)S(1)} %stack.65.scal_ref, bf16[4,2,128,1024]{3,2,1,0:T(8,128)(2,1)} %bitcast.24.refs_0_, bf16[4,2,128,1024]{3,2,1,0:T(8,128)(2,1)} %bitcast.25.refs_1_, bf16[1024,1024]{1,0:T(8,128)(2,1)S(1)} %multiply_convert_fusion.1.refs_2_, bf16[1024,1024]{1,0:T(8,128)(2,1)S(1)} %multiply_convert_fusion.refs_3_), custom_call_target="tpu_custom_call" | custom-call | flops 2147483648 | bytes 8388608 | tf_op jit(solution)/shard_map/pallas_call | solution.py:135
  90.9 2.3 constant_dynamic-slice_fusion
  94.4 18.0 %collective-permute-done = bf16[1024,1024]{1,0:T(8,128)(2,1)} collective-permute-done((bf16[1024,1024]{1,0:T(8,128)(2,1)}, bf16[1024,1024]{1,0:T(8,128)(2,1)}, u32[]{:S(2)}, u32[]{:S(2)}) %collective-permute-start) | collective-permute-done | bytes 2097184 | tf_op jit(solution)/shard_map/ppermute | solution.py:239
  112.4 2.3 constant_dynamic-slice_fusion.1
  117.4 5.3 %shard_map.74 = (f32[4,128,256]{2,1,0:T(8,128)S(1)}, f32[4,128,256]{2,1,0:T(8,128)S(1)}, f32[4,128,256]{2,1,0:T(8,128)S(1)}, f32[4,128,256]{2,1,0:T(8,128)S(1)}) custom-call(s32[5]{0:T(128)S(1)} %stack.31.scal_ref, bf16[4,2,128,1024]{3,2,1,0:T(8,128)(2,1)} %bitcast.24.refs_0_, bf16[4,2,128,1024]{3,2,1,0:T(8,128)(2,1)} %bitcast.25.refs_1_, ...), custom_call_target="tpu_custom_call" | custom-call | flops 2147483648 | bytes 8388608 | tf_op jit(solution)/shard_map/pallas_call | solution.py:135
  122.8 2.8 %fusion.9 = (f32[4,128,256]{2,1,0:T(8,128)}, f32[4,128,256]{2,1,0:T(8,128)}, f32[4,128,256]{2,1,0:T(8,128)}) fusion(f32[4,128,256]{2,1,0:T(8,128)S(1)} %get-tuple-element.26, f32[4,4,128,256]{3,2,1,0:T(8,128)} %collective-permute-done.12, f32[4,128,256]{2,1,0:T(8,128)S(1)} %get-tuple-element.28, f32[4,128,256]{2,1,0:T(8,128)S(1)} %get-tuple-element.27), kind=kLoop, calls=%fused_computation.24 | loop fusion | flops 393216 | bytes 4718592 | tf_op jit(solution)/shard_map/add | solution.py:252
  126.8 2.5 collective-permute-start.15
  130.5 4.4 %collective-permute-done.21 = bf16[1024,512]{1,0:T(8,128)(2,1)} collective-permute-done((bf16[1024,512]{1,0:T(8,128)(2,1)}, bf16[1024,512]{1,0:T(8,128)(2,1)}, u32[]{:S(2)}, u32[]{:S(2)}) %collective-permute-start.21) | collective-permute-done | bytes 1048608 | tf_op jit(solution)/shard_map/ppermute | solution.py:243
  134.8 5.2 %shard_map.77 = f32[4,4,128,256]{3,2,1,0:T(8,128)} custom-call(s32[5]{0:T(128)S(1)} %stack.65.scal_ref, bf16[4,2,128,512]{3,2,1,0:T(8,128)(2,1)} %bitcast.37.refs_0_, bf16[4,2,128,512]{3,2,1,0:T(8,128)(2,1)S(1)} %bitcast.125, bf16[1024,1024]{1,0:T(8,128)(2,1)S(1)} %multiply_convert_fusion.1.refs_2_, bf16[1024,1024]{1,0:T(8,128)(2,1)S(1)} %copy-done.4), custom_call_target="tpu_custom_call" | custom-call | flops 1073741824 | bytes 5242880 | tf_op jit(solution)/shard_map/pallas_call | solution.py:135
  140.0 2.5 collective-permute-start.23
  144.9 8.3 %shard_map.73 = (f32[4,256,256]{2,1,0:T(8,128)S(1)}, f32[4,256,256]{2,1,0:T(8,128)S(1)}, f32[4,256,256]{2,1,0:T(8,128)S(1)}, f32[4,256,256]{2,1,0:T(8,128)S(1)}) custom-call(s32[5]{0:T(128)S(1)} %stack.30.scal_ref, bf16[4,1,256,1024]{3,2,1,0:T(8,128)(2,1)} %bitcast.9.refs_0_, bf16[4,1,256,1024]{3,2,1,0:T(8,128)(2,1)} %bitcast.14.refs_1_, ...), custom_call_target="tpu_custom_call" | custom-call | flops 4294967296 | bytes 12582912 | tf_op jit(solution)/shard_map/pallas_call | solution.py:135
  159.6 4.6 %collective-permute-done.18 = f32[128,256]{1,0:T(8,128)S(1)} collective-permute-done((f32[128,256]{1,0:T(8,128)S(1)}, f32[128,256]{1,0:T(8,128)S(1)}, u32[]{:S(2)}, u32[]{:S(2)}) %collective-permute-start.18) | collective-permute-done | bytes 131104 | tf_op jit(solution)/shard_map/ppermute | solution.py:169
  165.8 5.2 %collective-permute-done.17 = f32[128,256]{1,0:T(8,128)S(1)} collective-permute-done((f32[128,256]{1,0:T(8,128)S(1)}, f32[128,256]{1,0:T(8,128)S(1)}, u32[]{:S(2)}, u32[]{:S(2)}) %collective-permute-start.17) | collective-permute-done | bytes 131104 | tf_op jit(solution)/shard_map/ppermute | solution.py:169
  171.7 3.9 %shard_map.76 = (f32[4,128,256]{2,1,0:T(8,128)S(1)}, f32[4,128,256]{2,1,0:T(8,128)S(1)}, f32[4,128,256]{2,1,0:T(8,128)S(1)}, f32[4,128,256]{2,1,0:T(8,128)S(1)}) custom-call(s32[5]{0:T(128)S(1)} %stack.31.scal_ref, bf16[4,2,128,512]{3,2,1,0:T(8,128)(2,1)} %bitcast.37.refs_0_, bf16[4,2,128,512]{3,2,1,0:T(8,128)(2,1)S(1)} %bitcast.126, ...), custom_call_target="tpu_custom_call" | custom-call | flops 1073741824 | bytes 5242880 | tf_op jit(solution)/shard_map/pallas_call | solution.py:135
  183.9 3.5 %collective-permute-done.24 = f32[4,128,256]{2,1,0:T(8,128)S(1)} collective-permute-done((f32[4,128,256]{2,1,0:T(8,128)S(1)}, f32[4,128,256]{2,1,0:T(8,128)S(1)}, u32[]{:S(2)}, u32[]{:S(2)}) %collective-permute-start.24) | collective-permute-done | bytes 524320 | tf_op jit(solution)/shard_map/ppermute | solution.py:166
  189.5 3.5 %collective-permute-done.26 = f32[4,128,256]{2,1,0:T(8,128)S(1)} collective-permute-done((f32[4,128,256]{2,1,0:T(8,128)S(1)}, f32[4,128,256]{2,1,0:T(8,128)S(1)}, u32[]{:S(2)}, u32[]{:S(2)}) %collective-permute-start.26) | collective-permute-done | bytes 524320 | tf_op jit(solution)/shard_map/ppermute | solution.py:166
  199.6 4.6 %collective-permute-start.11 = (f32[256,256]{1,0:T(8,128)S(1)}, f32[256,256]{1,0:T(8,128)S(1)}, u32[]{:S(2)}, u32[]{:S(2)}) collective-permute-start(f32[256,256]{1,0:T(8,128)S(1)} %fusion.16), channel_id=1, source_target_pairs={{64,8},{73,9},{80,10},{89,11},{96,12},{105,13},{112,14},{121,15},{... | collective-permute-start | bytes 786440 | tf_op jit(solution)/shard_map/ppermute | solution.py:261
  204.2 26.5 %collective-permute-start.10 = (f32[256,256]{1,0:T(8,128)S(1)}, f32[256,256]{1,0:T(8,128)S(1)}, u32[]{:S(2)}, u32[]{:S(2)}) collective-permute-start(f32[256,256]{1,0:T(8,128)S(1)} %fusion.16), channel_id=1, source_target_pairs={{9,8},{8,9},{11,10},{10,11},{13,12},{12,13},{15,14},{14,15},{25,24... | collective-permute-start | bytes 786440 | tf_op jit(solution)/shard_map/ppermute | solution.py:261
  233.5 7.2 %collective-permute-done.19.refs_4_ = f32[128,256]{1,0:T(8,128)S(1)} collective-permute-done((f32[128,256]{1,0:T(8,128)S(1)}, f32[128,256]{1,0:T(8,128)S(1)}, u32[]{:S(2)}, u32[]{:S(2)}) %collective-permute-start.19) | collective-permute-done | bytes 131104 | tf_op jit(solution)/shard_map/ppermute | solution.py:261
  240.8 6.6 %collective-permute-start.33 = (f32[128,256]{1,0:T(8,128)S(1)}, f32[128,256]{1,0:T(8,128)S(1)}, u32[]{:S(2)}, u32[]{:S(2)}) collective-permute-start(f32[128,256]{1,0:T(8,128)S(1)} %fusion.19), channel_id=1, source_target_pairs={{1,0},{9,1},{17,2},{25,3},{33,4},{41,5},{49,6},{57,7},{3,16},{11,1... | collective-permute-start | bytes 393224 | tf_op jit(solution)/shard_map/ppermute | solution.py:261
  248.7 3.0 %collective-permute-start.31 = (f32[128,256]{1,0:T(8,128)S(1)}, f32[128,256]{1,0:T(8,128)S(1)}, u32[]{:S(2)}, u32[]{:S(2)}) collective-permute-start(f32[128,256]{1,0:T(8,128)S(1)} %fusion.19), channel_id=1, source_target_pairs={{9,0},{1,1},{11,2},{3,3},{13,4},{5,5},{15,6},{7,7},{25,16},{17,17}... | collective-permute-start | bytes 393224 | tf_op jit(solution)/shard_map/ppermute | solution.py:261
  253.7 10.4 %collective-permute-done.32.refs_8_ = f32[128,256]{1,0:T(8,128)S(1)} collective-permute-done((f32[128,256]{1,0:T(8,128)S(1)}, f32[128,256]{1,0:T(8,128)S(1)}, u32[]{:S(2)}, u32[]{:S(2)}) %collective-permute-start.32) | collective-permute-done | bytes 131104 | tf_op jit(solution)/shard_map/ppermute | solution.py:261
  265.4 2.4 shard_map.78
  (111 shorter events, 47.8 us)
Async XLA Ops:
  8.4 36.3 %all-to-all-start.1 = ((bf16[32,32,1024]{2,0,1:T(8,128)(2,1)}), bf16[32,32,1024]{2,0,1:T(8,128)(2,1)}, u32[]{:S(2)}, u32[]{:S(2)}) async-start(bf16[32,32,1024]{2,0,1:T(8,128)(2,1)} %bitcast.130), calls=%async_computation.1 | async-start | bytes 4194304 | tf_op jit(solution)/shard_map/all_to_all | solution.py:233
  44.7 34.8 %all-to-all-start = ((bf16[32,32,1024]{2,0,1:T(8,128)(2,1)}), bf16[32,32,1024]{2,0,1:T(8,128)(2,1)}, u32[]{:S(2)}, u32[]{:S(2)}) async-start(bf16[32,32,1024]{2,0,1:T(8,128)(2,1)} %bitcast.129), calls=%async_computation | async-start | bytes 4194304 | tf_op jit(solution)/shard_map/all_to_all | solution.py:233
  64.3 26.5 %collective-permute-start.1 = (bf16[1024,1024]{1,0:T(8,128)(2,1)}, bf16[1024,1024]{1,0:T(8,128)(2,1)}, u32[]{:S(2)}, u32[]{:S(2)}) collective-permute-start(bf16[1024,1024]{1,0:T(8,128)(2,1)} %bitcast.12), channel_id=1, source_target_pairs={{64,0},{73,1},{8,64},{1,65},{72,8},{65,9},{0,72},{9,73},{66,2},{75... | collective-permute-start | bytes 6291464 | tf_op jit(solution)/shard_map/ppermute | solution.py:239
  79.5 32.9 %collective-permute-start = (bf16[1024,1024]{1,0:T(8,128)(2,1)}, bf16[1024,1024]{1,0:T(8,128)(2,1)}, u32[]{:S(2)}, u32[]{:S(2)}) collective-permute-start(bf16[1024,1024]{1,0:T(8,128)(2,1)} %bitcast.7), channel_id=1, source_target_pairs={{64,0},{73,1},{8,64},{1,65},{72,8},{65,9},{0,72},{9,73},{66,2},{75... | collective-permute-start | bytes 6291464 | tf_op jit(solution)/shard_map/ppermute | solution.py:239
  90.9 31.9 %collective-permute-start.12 = (f32[4,4,128,256]{3,2,1,0:T(8,128)}, f32[4,4,128,256]{3,2,1,0:T(8,128)}, u32[]{:S(2)}, u32[]{:S(2)}) collective-permute-start(f32[4,4,128,256]{3,2,1,0:T(8,128)} %shard_map.75), channel_id=1, source_target_pairs={{0,1},{1,0},{2,3},{3,2},{4,5},{5,4},{6,7},{7,6},{8,9},{9,8},{10,11... | collective-permute-start | bytes 6291464 | tf_op jit(solution)/shard_map/ppermute | solution.py:174
  93.2 37.3 %collective-permute-start.22 = (bf16[1024,512]{1,0:T(8,128)(2,1)}, bf16[1024,512]{1,0:T(8,128)(2,1)S(1)}, u32[]{:S(2)}, u32[]{:S(2)}) collective-permute-start(bf16[1024,512]{1,0:T(8,128)(2,1)} %constant_dynamic-slice_fusion), channel_id=1, source_target_pairs={{64,0},{73,1},{8,64},{1,65},{72,8},{65,9},{0,72},{9,73},{66,2},{75... | collective-permute-start | bytes 3145736 | tf_op jit(solution)/shard_map/ppermute | solution.py:243
  114.6 20.2 %collective-permute-start.21 = (bf16[1024,512]{1,0:T(8,128)(2,1)}, bf16[1024,512]{1,0:T(8,128)(2,1)}, u32[]{:S(2)}, u32[]{:S(2)}) collective-permute-start(bf16[1024,512]{1,0:T(8,128)(2,1)} %constant_dynamic-slice_fusion.1), channel_id=1, source_target_pairs={{64,0},{73,1},{8,64},{1,65},{72,8},{65,9},{0,72},{9,73},{66,2},{75... | collective-permute-start | bytes 3145736 | tf_op jit(solution)/shard_map/ppermute | solution.py:243
  125.6 17.0 %collective-permute-start.13 = (f32[4,128,256]{2,1,0:T(8,128)}, f32[4,128,256]{2,1,0:T(8,128)}, u32[]{:S(2)}, u32[]{:S(2)}) collective-permute-start(f32[4,128,256]{2,1,0:T(8,128)} %get-tuple-element.36), channel_id=1, source_target_pairs={{0,2},{1,17},{2,4},{3,19},{4,6},{5,21},{6,0},{7,23},{16,18},{17,33... | collective-permute-start | bytes 1572872 | tf_op jit(solution)/shard_map/ppermute | solution.py:166
  126.8 15.7 %collective-permute-start.15 = (f32[4,128,256]{2,1,0:T(8,128)}, f32[4,128,256]{2,1,0:T(8,128)}, u32[]{:S(2)}, u32[]{:S(2)}) collective-permute-start(f32[4,128,256]{2,1,0:T(8,128)} %get-tuple-element.37), channel_id=1, source_target_pairs={{0,4},{1,33},{2,6},{3,35},{4,0},{5,37},{6,2},{7,39},{16,20},{17,49... | collective-permute-start | bytes 1572872 | tf_op jit(solution)/shard_map/ppermute | solution.py:166
  129.3 13.2 %collective-permute-start.14 = (f32[4,128,256]{2,1,0:T(8,128)}, f32[4,128,256]{2,1,0:T(8,128)}, u32[]{:S(2)}, u32[]{:S(2)}) collective-permute-start(f32[4,128,256]{2,1,0:T(8,128)} %get-tuple-element.38), channel_id=1, source_target_pairs={{0,6},{1,49},{2,0},{3,51},{4,2},{5,53},{6,4},{7,55},{16,22},{17,1}... | collective-permute-start | bytes 1572872 | tf_op jit(solution)/shard_map/ppermute | solution.py:166
  140.0 35.6 %collective-permute-start.23 = (f32[4,4,128,256]{3,2,1,0:T(8,128)}, f32[4,4,128,256]{3,2,1,0:T(8,128)}, u32[]{:S(2)}, u32[]{:S(2)}) collective-permute-start(f32[4,4,128,256]{3,2,1,0:T(8,128)} %shard_map.77), channel_id=1, source_target_pairs={{0,1},{1,0},{2,3},{3,2},{4,5},{5,4},{6,7},{7,6},{8,9},{9,8},{10,11... | collective-permute-start | bytes 6291464 | tf_op jit(solution)/shard_map/ppermute | solution.py:174
  144.6 12.9 %collective-permute-start.16 = (f32[128,256]{1,0:T(8,128)S(1)}, f32[128,256]{1,0:T(8,128)S(1)}, u32[]{:S(2)}, u32[]{:S(2)}) collective-permute-start(f32[128,256]{1,0:T(8,128)S(1)} %get-tuple-element.45), channel_id=1, source_target_pairs={{0,16},{1,3},{2,18},{3,5},{4,20},{5,7},{6,22},{7,1},{16,32},{17,19... | collective-permute-start | bytes 393224 | tf_op jit(solution)/shard_map/ppermute | solution.py:169
  153.2 24.1 %collective-permute-start.2 = (f32[4,256,256]{2,1,0:T(8,128)S(1)}, f32[4,256,256]{2,1,0:T(8,128)S(1)}, u32[]{:S(2)}, u32[]{:S(2)}) collective-permute-start(f32[4,256,256]{2,1,0:T(8,128)S(1)} %get-tuple-element.22), channel_id=1, source_target_pairs={{0,2},{1,17},{2,4},{3,19},{4,6},{5,21},{6,0},{7,23},{16,18},{17,33... | collective-permute-start | bytes 3145736 | tf_op jit(solution)/shard_map/ppermute | solution.py:166
  154.5 24.8 %collective-permute-start.3 = (f32[4,256,256]{2,1,0:T(8,128)S(1)}, f32[4,256,256]{2,1,0:T(8,128)S(1)}, u32[]{:S(2)}, u32[]{:S(2)}) collective-permute-start(f32[4,256,256]{2,1,0:T(8,128)S(1)} %get-tuple-element.23), channel_id=1, source_target_pairs={{0,6},{1,49},{2,0},{3,51},{4,2},{5,53},{6,4},{7,55},{16,22},{17,1}... | collective-permute-start | bytes 3145736 | tf_op jit(solution)/shard_map/ppermute | solution.py:166
  155.9 26.2 %collective-permute-start.4 = (f32[4,256,256]{2,1,0:T(8,128)S(1)}, f32[4,256,256]{2,1,0:T(8,128)S(1)}, u32[]{:S(2)}, u32[]{:S(2)}) collective-permute-start(f32[4,256,256]{2,1,0:T(8,128)S(1)} %get-tuple-element.24), channel_id=1, source_target_pairs={{0,4},{1,33},{2,6},{3,35},{4,0},{5,37},{6,2},{7,39},{16,20},{17,49... | collective-permute-start | bytes 3145736 | tf_op jit(solution)/shard_map/ppermute | solution.py:166
  171.0 33.2 %collective-permute-start.20 = (f32[128,256]{1,0:T(8,128)S(1)}, f32[128,256]{1,0:T(8,128)S(1)}, u32[]{:S(2)}, u32[]{:S(2)}) collective-permute-start(f32[128,256]{1,0:T(8,128)S(1)} %fusion.22), channel_id=1, source_target_pairs={{1,0},{9,1},{3,2},{11,3},{5,4},{13,5},{7,6},{15,7},{17,16},{25,17}... | collective-permute-start | bytes 393224 | tf_op jit(solution)/shard_map/ppermute | solution.py:261
  177.2 10.3 %collective-permute-start.24 = (f32[4,128,256]{2,1,0:T(8,128)S(1)}, f32[4,128,256]{2,1,0:T(8,128)S(1)}, u32[]{:S(2)}, u32[]{:S(2)}) collective-permute-start(f32[4,128,256]{2,1,0:T(8,128)S(1)} %get-tuple-element.33), channel_id=1, source_target_pairs={{0,2},{1,17},{2,4},{3,19},{4,6},{5,21},{6,0},{7,23},{16,18},{17,33... | collective-permute-start | bytes 1572872 | tf_op jit(solution)/shard_map/ppermute | solution.py:166
  177.3 15.7 %collective-permute-start.26 = (f32[4,128,256]{2,1,0:T(8,128)S(1)}, f32[4,128,256]{2,1,0:T(8,128)S(1)}, u32[]{:S(2)}, u32[]{:S(2)}) collective-permute-start(f32[4,128,256]{2,1,0:T(8,128)S(1)} %get-tuple-element.34), channel_id=1, source_target_pairs={{0,4},{1,33},{2,6},{3,35},{4,0},{5,37},{6,2},{7,39},{16,20},{17,49... | collective-permute-start | bytes 1572872 | tf_op jit(solution)/shard_map/ppermute | solution.py:166
  179.3 15.0 %collective-permute-start.25 = (f32[4,128,256]{2,1,0:T(8,128)S(1)}, f32[4,128,256]{2,1,0:T(8,128)S(1)}, u32[]{:S(2)}, u32[]{:S(2)}) collective-permute-start(f32[4,128,256]{2,1,0:T(8,128)S(1)} %get-tuple-element.35), channel_id=1, source_target_pairs={{0,6},{1,49},{2,0},{3,51},{4,2},{5,53},{6,4},{7,55},{16,22},{17,1}... | collective-permute-start | bytes 1572872 | tf_op jit(solution)/shard_map/ppermute | solution.py:166
  182.6 14.5 %collective-permute-start.5 = (f32[256,256]{1,0:T(8,128)S(1)}, f32[256,256]{1,0:T(8,128)S(1)}, u32[]{:S(2)}, u32[]{:S(2)}) collective-permute-start(f32[256,256]{1,0:T(8,128)S(1)} %get-tuple-element.39), channel_id=1, source_target_pairs={{0,16},{1,3},{2,18},{3,5},{4,20},{5,7},{6,22},{7,1},{16,32},{17,19... | collective-permute-start | bytes 786440 | tf_op jit(solution)/shard_map/ppermute | solution.py:169
  187.4 10.6 %collective-permute-start.7 = (f32[256,256]{1,0:T(8,128)S(1)}, f32[256,256]{1,0:T(8,128)S(1)}, u32[]{:S(2)}, u32[]{:S(2)}) collective-permute-start(f32[256,256]{1,0:T(8,128)S(1)} %get-tuple-element.40), channel_id=1, source_target_pairs={{0,32},{1,5},{2,34},{3,7},{4,36},{5,1},{6,38},{7,3},{16,48},{17,21... | collective-permute-start | bytes 786440 | tf_op jit(solution)/shard_map/ppermute | solution.py:169
  195.6 35.2 %collective-permute-start.27 = (f32[128,256]{1,0:T(8,128)S(1)}, f32[128,256]{1,0:T(8,128)S(1)}, u32[]{:S(2)}, u32[]{:S(2)}) collective-permute-start(f32[128,256]{1,0:T(8,128)S(1)} %get-tuple-element.42), channel_id=1, source_target_pairs={{0,16},{1,3},{2,18},{3,5},{4,20},{5,7},{6,22},{7,1},{16,32},{17,19... | collective-permute-start | bytes 393224 | tf_op jit(solution)/shard_map/ppermute | solution.py:169
  197.1 34.4 %collective-permute-start.29 = (f32[128,256]{1,0:T(8,128)S(1)}, f32[128,256]{1,0:T(8,128)S(1)}, u32[]{:S(2)}, u32[]{:S(2)}) collective-permute-start(f32[128,256]{1,0:T(8,128)S(1)} %get-tuple-element.43), channel_id=1, source_target_pairs={{0,32},{1,5},{2,34},{3,7},{4,36},{5,1},{6,38},{7,3},{16,48},{17,21... | collective-permute-start | bytes 393224 | tf_op jit(solution)/shard_map/ppermute | solution.py:169
  198.0 34.7 %collective-permute-start.28 = (f32[128,256]{1,0:T(8,128)S(1)}, f32[128,256]{1,0:T(8,128)S(1)}, u32[]{:S(2)}, u32[]{:S(2)}) collective-permute-start(f32[128,256]{1,0:T(8,128)S(1)} %get-tuple-element.44), channel_id=1, source_target_pairs={{0,48},{1,7},{2,50},{3,1},{4,52},{5,3},{6,54},{7,5},{16,0},{17,23}... | collective-permute-start | bytes 393224 | tf_op jit(solution)/shard_map/ppermute | solution.py:169
  199.6 47.8 %collective-permute-start.11 = (f32[256,256]{1,0:T(8,128)S(1)}, f32[256,256]{1,0:T(8,128)S(1)}, u32[]{:S(2)}, u32[]{:S(2)}) collective-permute-start(f32[256,256]{1,0:T(8,128)S(1)} %fusion.16), channel_id=1, source_target_pairs={{64,8},{73,9},{80,10},{89,11},{96,12},{105,13},{112,14},{121,15},{... | collective-permute-start | bytes 786440 | tf_op jit(solution)/shard_map/ppermute | solution.py:261
  204.2 44.5 %collective-permute-start.10 = (f32[256,256]{1,0:T(8,128)S(1)}, f32[256,256]{1,0:T(8,128)S(1)}, u32[]{:S(2)}, u32[]{:S(2)}) collective-permute-start(f32[256,256]{1,0:T(8,128)S(1)} %fusion.16), channel_id=1, source_target_pairs={{9,8},{8,9},{11,10},{10,11},{13,12},{12,13},{15,14},{14,15},{25,24... | collective-permute-start | bytes 786440 | tf_op jit(solution)/shard_map/ppermute | solution.py:261
  230.8 20.9 %collective-permute-start.9 = (f32[256,256]{1,0:T(8,128)S(1)}, f32[256,256]{1,0:T(8,128)S(1)}, u32[]{:S(2)}, u32[]{:S(2)}) collective-permute-start(f32[256,256]{1,0:T(8,128)S(1)} %fusion.16), channel_id=1, source_target_pairs={{65,8},{72,9},{81,10},{88,11},{97,12},{104,13},{113,14},{120,15},{... | collective-permute-start | bytes 786440 | tf_op jit(solution)/shard_map/ppermute | solution.py:261
  232.8 20.9 %collective-permute-start.8 = (f32[256,256]{1,0:T(8,128)S(1)}, f32[256,256]{1,0:T(8,128)S(1)}, u32[]{:S(2)}, u32[]{:S(2)}) collective-permute-start(f32[256,256]{1,0:T(8,128)S(1)} %fusion.16), channel_id=1, source_target_pairs={{0,8},{1,9},{2,10},{3,11},{4,12},{5,13},{6,14},{7,15},{16,24},{17,... | collective-permute-start | bytes 786440 | tf_op jit(solution)/shard_map/ppermute | solution.py:261
  240.8 12.9 %collective-permute-start.33 = (f32[128,256]{1,0:T(8,128)S(1)}, f32[128,256]{1,0:T(8,128)S(1)}, u32[]{:S(2)}, u32[]{:S(2)}) collective-permute-start(f32[128,256]{1,0:T(8,128)S(1)} %fusion.19), channel_id=1, source_target_pairs={{1,0},{9,1},{17,2},{25,3},{33,4},{41,5},{49,6},{57,7},{3,16},{11,1... | collective-permute-start | bytes 393224 | tf_op jit(solution)/shard_map/ppermute | solution.py:261
  247.4 16.6 %collective-permute-start.32 = (f32[128,256]{1,0:T(8,128)S(1)}, f32[128,256]{1,0:T(8,128)S(1)}, u32[]{:S(2)}, u32[]{:S(2)}) collective-permute-start(f32[128,256]{1,0:T(8,128)S(1)} %fusion.19), channel_id=1, source_target_pairs={{0,0},{8,1},{16,2},{24,3},{32,4},{40,5},{48,6},{56,7},{2,16},{10,1... | collective-permute-start | bytes 393224 | tf_op jit(solution)/shard_map/ppermute | solution.py:261
  248.7 15.3 %collective-permute-start.31 = (f32[128,256]{1,0:T(8,128)S(1)}, f32[128,256]{1,0:T(8,128)S(1)}, u32[]{:S(2)}, u32[]{:S(2)}) collective-permute-start(f32[128,256]{1,0:T(8,128)S(1)} %fusion.19), channel_id=1, source_target_pairs={{9,0},{1,1},{11,2},{3,3},{13,4},{5,5},{15,6},{7,7},{25,16},{17,17}... | collective-permute-start | bytes 393224 | tf_op jit(solution)/shard_map/ppermute | solution.py:261
  251.7 12.3 %collective-permute-start.30 = (f32[128,256]{1,0:T(8,128)S(1)}, f32[128,256]{1,0:T(8,128)S(1)}, u32[]{:S(2)}, u32[]{:S(2)}) collective-permute-start(f32[128,256]{1,0:T(8,128)S(1)} %fusion.19), channel_id=1, source_target_pairs={{8,0},{0,1},{10,2},{2,3},{12,4},{4,5},{14,6},{6,7},{24,16},{16,17}... | collective-permute-start | bytes 393224 | tf_op jit(solution)/shard_map/ppermute | solution.py:261
  (21 other events, 327.5 us)
where the time goes:
time: 269 us; the launch traced here: 268 us
  waiting for transfers between devices  101 us (38%)
  starting transfers between devices  90.8 us (34%)
  Pallas kernels  31.8 us (12%)
  local copies, waits for them, and re-layouts  23.7 us (9%)
  other arithmetic  19.9 us (7%)
    ppermute x10, starting transfers between devices, fetch(): return lax.ppermute(value, AXES, homes(place))  46.7 us
    all_to_all x2, waiting for transfers between devices, body(): lax.all_to_all(packed, PLANE, split_axis=1, concat_axis=0, tiled=True)  41 us
    pallas_call x5, Pallas kernels, tile_products(): pl.pallas_call(functools.partial(tile_kernel, chunks=chunks, n_out=len(ou...  29.4 us
    ppermute x2, waiting for transfers between devices, body(): near.append(lax.ppermute(scaled[j], RING, to_ring_neighbour()))  18 us
    ppermute x10, waiting for transfers between devices, fetch(): return lax.ppermute(value, AXES, homes(place))  17.6 us
    all_to_all x2, starting transfers between devices, body(): lax.all_to_all(packed, PLANE, split_axis=1, concat_axis=0, tiled=True)  15.7 us
    ppermute x9, starting transfers between devices, reduce_plane(): total = total + lax.ppermute(strips[shift], PLANE, plane_shift(shift, True))  12.3 us
    gather x1, local copies, waits for them, and re-layouts, body(): column_var = cell_var[positions]  11.8 us
  transfers between devices with their start and end apart: 36, of which 12 were waited for; matrix products, arithmetic and copies ran while one was open for 12% of the time, Pallas kernels for 11%

commit v1 on v0

v1 whole, which is shorter than its diff:
```python
import functools

import jax
import jax.numpy as jnp
from jax import lax
from jax.experimental import pallas as pl
from jax.experimental.pallas import tpu as pltpu
from jax.sharding import Mesh, PartitionSpec as P


AXES = ("xl", "z", "xh", "y", "core")
SIZES = (2, 4, 2, 4, 2)
PLANE = ("z", "y", "core")
RING = ("xl", "xh", "core")
PARTS = (5, 3)
CHUNKS = len(PARTS)
INTERPRET = False
VMEM_GRANT = 60 * 2**20


def row_weights(row_period, row_site, period_err, site_err):
    period_hit = row_period[:, None] == jnp.arange(period_err.shape[0], dtype=jnp.int32)[None, :]
    site_hit = row_site[:, None] == jnp.arange(site_err.shape[0], dtype=jnp.int32)[None, :]
    period_scale = jnp.sum(jnp.where(period_hit, period_err[None, :], 0.0), axis=1)
    site_scale = jnp.sum(jnp.where(site_hit, site_err[None, :], 0.0), axis=1)
    return 1.0 / jnp.sqrt(period_scale * period_scale + site_scale * site_scale)


def pack_kernel(period_ref, site_ref, period_err_ref, site_err_ref, data_ref, out_ref, weight_ref):
    rows = data_ref.shape[0]
    blocks, _, depth = out_ref.shape

    @pl.when(pl.program_id(0) == 0)
    def _():
        def iota(shape, axis):
            return lax.broadcasted_iota(jnp.int32, shape, axis)

        def looked_up(index_ref, table_ref):
            square = (rows, rows)
            diagonal = iota(square, 0) == iota(square, 1)
            index = jnp.sum(
                jnp.where(diagonal, index_ref[...].astype(jnp.float32), 0.0), axis=1, keepdims=True
            ).astype(jnp.int32)
            hit = index == iota((rows, table_ref.shape[1]), 1)
            return jnp.sum(jnp.where(hit, table_ref[...], 0.0), axis=1, keepdims=True)

        period_scale = looked_up(period_ref, period_err_ref)
        site_scale = looked_up(site_ref, site_err_ref)
        weight = 1.0 / jnp.sqrt(period_scale * period_scale + site_scale * site_scale)
        weight_ref[...] = jnp.broadcast_to(weight, weight_ref.shape)

    weight = weight_ref[:, :1]
    for block in range(blocks):
        data = data_ref[:, block * depth : (block + 1) * depth]
        out_ref[block] = (weight * data).astype(jnp.bfloat16)


def pack_first(sensitivity, row_period, row_site, period_err, site_err, depth):
    rows = sensitivity.shape[0]
    steps = 4
    tables = [a[None, :] for a in (row_period, row_site, period_err, site_err)]
    return pl.pallas_call(
        pack_kernel,
        out_shape=jax.ShapeDtypeStruct((32, rows, depth), jnp.bfloat16),
        grid=(steps,),
        in_specs=[pl.BlockSpec(a.shape, lambda i: (0, 0)) for a in tables]
        + [pl.BlockSpec((rows, 32 // steps * depth), lambda i: (0, i))],
        out_specs=pl.BlockSpec((32 // steps, rows, depth), lambda i: (i, 0, 0)),
        scratch_shapes=[pltpu.VMEM((rows, 128), jnp.float32)],
        compiler_params=pltpu.CompilerParams(
            dimension_semantics=("arbitrary",), vmem_limit_bytes=VMEM_GRANT
        ),
        cost_estimate=pl.CostEstimate(
            flops=32 * rows * depth, bytes_accessed=32 * rows * depth * 6, transcendentals=0
        ),
        interpret=INTERPRET,
    )(*tables, sensitivity)


def flat(xl, z, xh, y, core):
    return (((xl * 4 + z) * 2 + xh) * 4 + y) * 2 + core


def ring_index(x, core):
    return ((x % 2) * 2 + x // 2) * 2 + core


def to_ring_neighbour():
    pairs = []
    for x in range(4):
        pairs.append((ring_index((x + 1) % 4, 0), ring_index(x, 0)))
        pairs.append((ring_index((x - 1) % 4, 1), ring_index(x, 1)))
    return pairs


def plane_shift(shift, first):
    pairs = []
    for z in range(4):
        for y in range(4):
            for core in range(2):
                along_y = (core == 0) == first
                to_z, to_y = (z, (y + shift) % 4) if along_y else ((z + shift) % 4, y)
                pairs.append(((z * 4 + y) * 2 + core, (to_z * 4 + to_y) * 2 + core))
    return pairs


def homes(place):
    pairs = []
    for xl in range(2):
        for z in range(4):
            for xh in range(2):
                for y in range(4):
                    for core in range(2):
                        source = place(xl, z, xh, y, core)
                        if source is not None:
                            pairs.append((flat(*source), flat(xl, z, xh, y, core)))
    return pairs


def own_source(part):
    return lambda xl, z, xh, y, core: (xl, z, core, y, part) if xh == xl else None


def near_source(half, mirrored):
    def place(xl, z, xh, y, core):
        if xh == xl:
            return None
        forward = (2 * core + xh - (2 * half + xl)) % 4 == 1
        holder = 0 if forward else 1
        return (xh, y, core, z, 1 - holder) if mirrored else (xl, z, half, y, holder)

    return place


def far_source(half, mirrored):
    def place(xl, z, xh, y, core):
        if xh != xl:
            return None
        part, flip = far_role(xl, core, half, mirrored)
        return (xl, y, core, z, part) if flip else (xl, z, 1 - core, y, part)

    return place


def both(first, second):
    return lambda *device: first(*device) or second(*device)


def far_role(xl, core, half, mirrored):
    slot = (2 + (half ^ (1 - xl))) if mirrored else half
    return (((0, 0), (0, 1), (1, 0), (1, 1)), ((1, 1), (1, 0), (0, 0), (0, 1)))[core][slot]


def tile_kernel(scal_ref, *refs, chunks, n_out, based):
    lhs, rhs = refs[:chunks], refs[chunks : 2 * chunks]
    base = refs[2 * chunks] if based else None
    outs, scratch = refs[2 * chunks + based : 2 * chunks + based + n_out], refs[-1]
    c = pl.program_id(0)
    height, _ = scratch.shape[2:]
    total = None
    for a, b in zip(lhs, rhs):
        part = lax.dot_general(
            a[...].reshape(4 * height, a.shape[-1]),
            b[...],
            (((1,), (1,)), ((), ())),
            preferred_element_type=jnp.float32,
        )
        total = part if total is None else total + part
    across = lax.rem(c + 4 - scal_ref[1], 4)
    for r in range(4):
        down = lax.rem(r + 4 - scal_ref[0], 4)
        s = jnp.where(scal_ref[2] == 0, down, across)
        v = jnp.where(scal_ref[2] == 0, across, down)
        scratch[s, v] = total[r * height : (r + 1) * height]

    @pl.when(c == 3)
    def _():
        if n_out == 1:
            outs[0][...] = scratch[...]
        else:
            for i in range(4):
                outs[i][...] = scratch[i] + base[i] if based else scratch[i]


def tile_products(lhs, rhs, scalars, split=False, joined=False, windowed=False, base=None):
    rows = lhs[0].shape[0]
    depths = [a.shape[1] for a in lhs]
    tile = rows // 4
    height = tile // 2 if split else tile
    lhs = [a.reshape(4, tile // height, height, depth) for a, depth in zip(lhs, depths)]
    if joined:
        out_shape = [jax.ShapeDtypeStruct((4, 4, height, tile), jnp.float32)]
        out_specs = [pl.BlockSpec((4, 4, height, tile), lambda c, scal: (0, 0, 0, 0))]
    else:
        out_shape = [jax.ShapeDtypeStruct((4, height, tile), jnp.float32)] * 4
        out_specs = [pl.BlockSpec((4, height, tile), lambda c, scal: (0, 0, 0))] * 4
    lhs_specs = [
        pl.BlockSpec(
            (4, 1, height, depth),
            lambda c, scal: (0, scal[3], 0, 0),
            pipeline_mode=pl.Buffered(1),
        )
        for depth in depths
    ]
    rhs_specs = [
        pl.BlockSpec((tile, depth), lambda c, scal: (c, scal[4] if windowed else 0))
        for depth in depths
    ]
    extra = [] if base is None else [base]
    base_specs = [
        pl.BlockSpec(a.shape, lambda c, scal: (0, 0, 0, 0), pipeline_mode=pl.Buffered(1))
        for a in extra
    ]
    return pl.pallas_call(
        functools.partial(
            tile_kernel, chunks=len(lhs), n_out=len(out_shape), based=len(extra)
        ),
        out_shape=out_shape,
        grid_spec=pltpu.PrefetchScalarGridSpec(
            num_scalar_prefetch=1,
            grid=(4,),
            in_specs=lhs_specs + rhs_specs + base_specs,
            out_specs=out_specs,
            scratch_shapes=[pltpu.VMEM((4, 4, height, tile), jnp.float32)],
        ),
        compiler_params=pltpu.CompilerParams(
            dimension_semantics=("arbitrary",), vmem_limit_bytes=VMEM_GRANT
        ),
        cost_estimate=pl.CostEstimate(
            flops=2 * 16 * height * tile * sum(depths),
            bytes_accessed=16 * height * tile * 4 + (height * 4 + rows) * sum(depths) * 2,
            transcendentals=0,
        ),
        interpret=INTERPRET,
    )(scalars, *lhs, *rhs, *extra)


def reduce_plane(strips):
    total = strips[0]
    for shift in (1, 3, 2):
        total = total + lax.ppermute(strips[shift], PLANE, plane_shift(shift, True))
    tile = total[0]
    for shift in (1, 3, 2):
        tile = tile + lax.ppermute(total[shift], PLANE, plane_shift(shift, False))
    return tile


def swap_cores(value):
    return lax.ppermute(value, "core", [(0, 1), (1, 0)])


def finish_kernel(scal_ref, *refs):
    direct, mixed, far, own, out = refs[:2], refs[2:4], refs[4:6], refs[6:8], refs[8]
    height, tile = own[0].shape
    core, even, xl = scal_ref[2], scal_ref[5], scal_ref[6]

    @pl.when(even == 0)
    def _():
        for half in range(2):
            out[:, half * tile : (half + 1) * tile] = direct[half][...] + mixed[half][...].T

    for xl_at in range(2):
        for core_at in range(2):

            @pl.when((even == 1) & (xl == xl_at) & (core == core_at))
            def _(xl_at=xl_at, core_at=core_at):
                parts = {}
                for half in range(2):
                    parts[far_role(xl_at, core_at, half, 0)] = far[half]
                    parts[far_role(xl_at, core_at, half, 1)] = mixed[half]
                other = (1 - core_at) * tile
                for part in range(2):
                    rows = slice(part * height, (part + 1) * height)
                    out[rows, core_at * tile : (core_at + 1) * tile] = own[part][...]
                    mirrored = jnp.concatenate(
                        [parts[piece, 1][:height, rows].T for piece in range(2)], axis=1
                    )
                    out[rows, other : other + tile] = parts[part, 0][:height] + mirrored


def finish(scalars, *operands):
    tile = operands[0].shape[0]
    return pl.pallas_call(
        finish_kernel,
        out_shape=jax.ShapeDtypeStruct((tile, 2 * tile), jnp.float32),
        in_specs=[pl.BlockSpec(memory_space=pltpu.SMEM)]
        + [pl.BlockSpec(memory_space=pltpu.VMEM)] * len(operands),
        out_specs=pl.BlockSpec(memory_space=pltpu.VMEM),
        cost_estimate=pl.CostEstimate(
            flops=tile * tile * 2, bytes_accessed=tile * tile * 4 * 8, transcendentals=0
        ),
        interpret=INTERPRET,
    )(scalars, *operands)


def body(sensitivity, row_period, row_site, period_err, site_err, cell_var, cell_perm):
    xl, z, xh, y, core = (lax.axis_index(name).astype(jnp.int32) for name in AXES)
    x = 2 * xh + xl
    cells = cell_var.shape[0]
    rows = sensitivity.shape[0]
    depths = [cells // 32 * part // sum(PARTS) for part in PARTS]
    starts = [32 * sum(depths[:j]) for j in range(CHUNKS)]
    place = (z * 4 + y) * 2 + core
    positions = jnp.concatenate(
        [
            lax.dynamic_slice_in_dim(cell_perm, start + place * depth, depth)
            for start, depth in zip(starts, depths)
        ]
    )
    column_var = cell_var[positions]

    scaled = []
    for j, (start, depth) in enumerate(zip(starts, depths)):
        if j == 0:
            packed = pack_first(sensitivity, row_period, row_site, period_err, site_err, depth)
        else:
            weight = row_weights(row_period, row_site, period_err, site_err)[:, None]
            packed = (weight * sensitivity[:, start : start + 32 * depth]).astype(jnp.bfloat16)
            packed = packed.reshape(rows, 32, depth).transpose(1, 0, 2)
        moved = lax.all_to_all(packed, PLANE, split_axis=0, concat_axis=0, tiled=True)
        scaled.append(moved.reshape(32 * rows, depth))

    other_var = swap_cores(column_var)

    def weigh(rows_on_cells, var, j):
        piece = var[None, starts[j] // 32 : starts[j] // 32 + depths[j]]
        return (rows_on_cells.astype(jnp.float32) * piece).astype(jnp.bfloat16)

    window = x // 2
    target = lax.rem(x + jnp.where(core == 0, 3, 1), 4)
    weighted, near, far = [], [], []
    other, other_weighted, other_far = [], [], []
    for j, depth in enumerate(depths):
        near.append(lax.ppermute(scaled[j], RING, to_ring_neighbour()))
        other.append(swap_cores(scaled[j]))
        weighted.append(weigh(scaled[j], column_var, j))
        other_weighted.append(weigh(other[j], other_var, j))
        cut = lax.dynamic_slice_in_dim(near[j], (target // 2) * (depth // 2), depth // 2, 1)
        far.append(lax.ppermute(cut, RING, to_ring_neighbour()))
        other_far.append(swap_cores(far[j]))

    whole = jnp.stack([y, z, core, 0 * core, window, (xh == xl).astype(jnp.int32), xl])
    halved = jnp.stack([y, z, core, core, window])
    base = tile_products(
        [scaled[0], other[0]], [weighted[0], other_weighted[0]], halved, split=True, joined=True
    )[0]
    strips = tile_products(
        [scaled[1], other[1]], [weighted[1], other_weighted[1]], halved, split=True, base=base
    )
    own_tile = reduce_plane(strips)
    strips = tile_products(near, weighted, whole)
    near_tile = reduce_plane(strips)
    strips = tile_products(
        far + other_far, weighted + other_weighted, halved, split=True, windowed=True
    )
    far_tile = reduce_plane(strips)

    def fetch(value, place):
        return lax.ppermute(value, AXES, homes(place))

    own = [fetch(own_tile, own_source(part)) for part in (0, 1)]
    direct = [fetch(near_tile, near_source(half, False)) for half in (0, 1)]
    padded = jnp.concatenate([far_tile, far_tile], axis=0)
    odd = xl ^ xh ^ core
    chosen = [jnp.where(odd == half, near_tile, padded) for half in (0, 1)]
    mixed = [
        fetch(chosen[half], both(near_source(half, True), far_source(half, 1)))
        for half in (0, 1)
    ]
    two = [fetch(far_tile, far_source(half, 0)) for half in (0, 1)]
    return finish(whole, *direct, *mixed, *two, *own)


def solution(mesh):
    fine = Mesh(mesh.devices.reshape(SIZES), AXES)

    return jax.shard_map(
        body,
        mesh=fine,
        in_specs=(P(AXES, None), P(AXES), P(AXES), P(), P(), P(), P()),
        out_specs=P(("xh", "y", "core"), ("xl", "z")),
        check_vma=False,
    )
```

time: 269 us -> 250 us (0.929)
  the two profiles are of different devices: /device:TPU:31 before, /device:TPU:30 now
where the time goes in v1:
time: 250 us; the launch traced here: 249 us
  waiting for transfers between devices  87.7 us (35%)
  starting transfers between devices  76.9 us (31%)
  Pallas kernels  42.4 us (17%)
  local copies, waits for them, and re-layouts  23.8 us (10%)
  other arithmetic  18 us (7%)
    all_to_all x2, waiting for transfers between devices, body(): lax.all_to_all(packed, PLANE, split_axis=0, concat_axis=0, tiled=True)  45.3 us
    pallas_call x4, Pallas kernels, tile_products(): pl.pallas_call(functools.partial(tile_kernel, chunks=len(lhs), n_out=len(...  35.2 us
    ppermute x8, starting transfers between devices, fetch(): return lax.ppermute(value, AXES, homes(place))  26.1 us
    ppermute x9, starting transfers between devices, reduce_plane(): tile = tile + lax.ppermute(total[shift], PLANE, plane_shift(shift, False))  18.5 us
    all_to_all x2, starting transfers between devices, body(): lax.all_to_all(packed, PLANE, split_axis=0, concat_axis=0, tiled=True)  17.5 us
    ppermute x9, waiting for transfers between devices, reduce_plane(): total = total + lax.ppermute(strips[shift], PLANE, plane_shift(shift, True))  13.2 us
    ppermute x8, waiting for transfers between devices, fetch(): return lax.ppermute(value, AXES, homes(place))  12.4 us
    gather x1, local copies, waits for them, and re-layouts, body(): column_var = cell_var[positions]  11.8 us
  transfers between devices with their start and end apart: 37, of which 11 were waited for; matrix products, arithmetic and copies ran while one was open for 16% of the time, Pallas kernels for 14%

profile of v1, /device:TPU:30, one launch (start us, length us, event | category | flops | bytes accessed | tf_op | source)
XLA Modules:
  0.0 249.3 jit_solution(12764410155116540849)
XLA Ops:
  0.0 5.0 %shard_map.73 = bf16[32,32,1280]{2,1,0:T(8,128)(2,1)} custom-call(s32[1,32]{1,0:T(1,128)} %bitcast.93, s32[1,32]{1,0:T(1,128)} %bitcast.91, f32[1,32]{1,0:T(1,128)} %bitcast.94, f32[1,128]{1,0:T(1,128)} %bitcast.92, f32[32,65536]{1,0:T(8,128)} %data_ref.1), custom_call_target="tpu_custom_call" | custom-call | flops 1310720 | bytes 7864320 | tf_op jit(solution)/shard_map/pallas_call | solution.py:62
  5.0 8.5 %all-to-all-start = ((bf16[32,32,1280]{2,1,0:T(8,128)(2,1)}), bf16[32,32,1280]{2,1,0:T(8,128)(2,1)S(1)}, u32[]{:S(2)}, u32[]{:S(2)}) async-start(bf16[32,32,1280]{2,1,0:T(8,128)(2,1)} %shard_map.73), calls=%async_computation | async-start | bytes 5242880 | tf_op jit(solution)/shard_map/all_to_all | solution.py:320
  13.9 2.1 multiply_convert_fusion.4
  17.4 27.8 %all-to-all-done = bf16[32,32,1280]{2,1,0:T(8,128)(2,1)S(1)} async-done(((bf16[32,32,1280]{2,1,0:T(8,128)(2,1)}), bf16[32,32,1280]{2,1,0:T(8,128)(2,1)S(1)}, u32[]{:S(2)}, u32[]{:S(2)}) %all-to-all-start) | async-done | bytes 2621472 | tf_op jit(solution)/shard_map/all_to_all | solution.py:320
  45.2 9.0 %all-to-all-start.1 = ((bf16[32,32,768]{2,1,0:T(8,128)(2,1)}), bf16[32,32,768]{2,1,0:T(8,128)(2,1)}, u32[]{:S(2)}, u32[]{:S(2)}) async-start(bf16[32,32,768]{2,1,0:T(8,128)(2,1)} %bitcast.84), calls=%async_computation.1 | async-start | bytes 3145728 | tf_op jit(solution)/shard_map/all_to_all | solution.py:320
  56.7 17.5 %all-to-all-done.1 = bf16[32,32,768]{2,1,0:T(8,128)(2,1)} async-done(((bf16[32,32,768]{2,1,0:T(8,128)(2,1)}), bf16[32,32,768]{2,1,0:T(8,128)(2,1)}, u32[]{:S(2)}, u32[]{:S(2)}) %all-to-all-start.1) | async-done | bytes 1572896 | tf_op jit(solution)/shard_map/all_to_all | solution.py:320
  74.2 2.0 collective-permute-start.16
  77.1 11.8 %gather_fusion = f32[2048]{0:T(1024)S(1)} fusion(f32[65536]{0:T(1024)S(1)} %copy-done, s32[2048]{0:T(1024)S(1)} %broadcast_clamp_fusion), kind=kCustom, calls=%fused_computation | custom fusion | bytes 24576 | tf_op jit(solution)/shard_map/gather | solution.py:310
  90.1 2.8 %multiply_convert_fusion.3.refs_3_.refs_5_.refs_2_ = bf16[1024,768]{1,0:T(8,128)(2,1)} fusion(f32[768]{0:T(1024)S(1)} %slice.71, bf16[32,32,768]{2,1,0:T(8,128)(2,1)} %all-to-all-done.1), kind=kLoop, calls=%fused_computation.4 | loop fusion | flops 2359296 | bytes 3148800 | tf_op jit(solution)/shard_map/convert_element_type | solution.py:327
  93.0 2.1 multiply_convert_fusion.1.refs_2_.refs_4_
  95.1 9.0 %collective-permute-done.1 = bf16[1024,768]{1,0:T(8,128)(2,1)} collective-permute-done((bf16[1024,768]{1,0:T(8,128)(2,1)}, bf16[1024,768]{1,0:T(8,128)(2,1)}, u32[]{:S(2)}, u32[]{:S(2)}) %collective-permute-start.1) | collective-permute-done | bytes 1572896 | tf_op jit(solution)/shard_map/ppermute | solution.py:334
  104.1 2.1 constant_dynamic-slice_fusion
  106.2 2.6 %constant_dynamic-slice_fusion.1 = bf16[1024,640]{1,0:T(8,128)(2,1)} fusion(bf16[1024,1280]{1,0:T(8,128)(2,1)} %collective-permute-done, s32[]{:T(128)S(6)} %select_n.66), kind=kLoop, calls=%fused_computation.44 | loop fusion | bytes 2621444 | tf_op jit(solution)/shard_map/dynamic_slice | solution.py:338
  109.0 2.9 %multiply_convert_fusion.2.refs_7_.refs_3_ = bf16[1024,768]{1,0:T(8,128)(2,1)} fusion(bf16[1024,768]{1,0:T(8,128)(2,1)} %collective-permute-done.16, f32[768]{0:T(1024)S(1)} %slice.77), kind=kLoop, calls=%fused_computation.3 | loop fusion | flops 2359296 | bytes 3148800 | tf_op jit(solution)/shard_map/convert_element_type | solution.py:327
  111.8 3.7 %multiply_convert_fusion.refs_6_.refs_3_ = bf16[1024,1280]{1,0:T(8,128)(2,1)} fusion(bf16[1024,1280]{1,0:T(8,128)(2,1)} %collective-permute-done.14, f32[1280]{0:T(1024)S(1)} %bitcast.90), kind=kLoop, calls=%fused_computation.1 | loop fusion | flops 3932160 | bytes 5248000 | tf_op jit(solution)/shard_map/convert_element_type | solution.py:327
  115.6 8.3 %shard_map.76.refs_4_ = f32[4,4,128,256]{3,2,1,0:T(8,128)} custom-call(s32[5]{0:T(128)} %stack.40.scal_ref, bf16[4,2,128,1280]{3,2,1,0:T(8,128)(2,1)} %bitcast.83, bf16[4,2,128,1280]{3,2,1,0:T(8,128)(2,1)} %bitcast.33.refs_1_, bf16[1024,1280]{1,0:T(8,128)(2,1)} %multiply_convert_fusion.1.refs_2_.refs_4_, bf16[1024,1280]{1,0:T(8,128)(2,1)} %multiply_convert_fusion.refs_6_.refs_3_), custom_call_target="tpu_custom_call" | custom-call | flops 2684354560 | bytes 9961472 | tf_op jit(solution)/shard_map/pallas_call | solution.py:214
  123.9 7.6 %shard_map.77 = (f32[4,128,256]{2,1,0:T(8,128)}, f32[4,128,256]{2,1,0:T(8,128)}, f32[4,128,256]{2,1,0:T(8,128)}, f32[4,128,256]{2,1,0:T(8,128)}) custom-call(s32[5]{0:T(128)} %stack.40.scal_ref, bf16[4,2,128,768]{3,2,1,0:T(8,128)(2,1)} %bitcast.30.refs_0_, bf16[4,2,128,768]{3,2,1,0:T(8,128)(2,1)} %bitcast.31.refs_1_, ...), custom_call_target="tpu_custom_call" | custom-call | flops 1610612736 | bytes 6815744 | tf_op jit(solution)/shard_map/pallas_call | solution.py:214
  136.3 11.0 %shard_map.74 = (f32[4,256,256]{2,1,0:T(8,128)}, f32[4,256,256]{2,1,0:T(8,128)}, f32[4,256,256]{2,1,0:T(8,128)}, f32[4,256,256]{2,1,0:T(8,128)}) custom-call(s32[7]{0:T(128)} %stack.39.scal_ref, bf16[4,1,256,1280]{3,2,1,0:T(8,128)(2,1)} %bitcast.12.refs_0_, bf16[4,1,256,768]{3,2,1,0:T(8,128)(2,1)} %bitcast.16.refs_1_, ...), custom_call_target="tpu_custom_call" | custom-call | flops 4294967296 | bytes 12582912 | tf_op jit(solution)/shard_map/pallas_call | solution.py:214
  147.3 2.2 collective-permute-start.2
  154.7 8.2 %shard_map.75 = (f32[4,128,256]{2,1,0:T(8,128)}, f32[4,128,256]{2,1,0:T(8,128)}, f32[4,128,256]{2,1,0:T(8,128)}, f32[4,128,256]{2,1,0:T(8,128)}) custom-call(s32[5]{0:T(128)} %stack.40.scal_ref, bf16[4,2,128,640]{3,2,1,0:T(8,128)(2,1)} %bitcast.22.refs_0_, bf16[4,2,128,384]{3,2,1,0:T(8,128)(2,1)} %bitcast.23.refs_1_, bf16[4,2,128,640]{3,2,1,0:T(8,128)(2,1)} %bitcast.86, ...), custom_call_target="tpu_custom_call" | custom-call | flops 2147483648 | bytes 8388608 | tf_op jit(solution)/shard_map/pallas_call | solution.py:214
  163.0 2.4 collective-permute-start.17
  165.9 7.5 %collective-permute-done.2 = f32[4,256,256]{2,1,0:T(8,128)} collective-permute-done((f32[4,256,256]{2,1,0:T(8,128)}, f32[4,256,256]{2,1,0:T(8,128)}, u32[]{:S(2)}, u32[]{:S(2)}) %collective-permute-start.2) | collective-permute-done | bytes 1048608 | tf_op jit(solution)/shard_map/ppermute | solution.py:241
  173.4 2.1 collective-permute-start.19
  175.5 2.8 %collective-permute-done.3 = f32[4,256,256]{2,1,0:T(8,128)} collective-permute-done((f32[4,256,256]{2,1,0:T(8,128)}, f32[4,256,256]{2,1,0:T(8,128)}, u32[]{:S(2)}, u32[]{:S(2)}) %collective-permute-start.3) | collective-permute-done | bytes 1048608 | tf_op jit(solution)/shard_map/ppermute | solution.py:241
  181.6 2.2 add_add_fusion
  183.8 6.8 %collective-permute-start.32 = (f32[128,256]{1,0:T(8,128)S(1)}, f32[128,256]{1,0:T(8,128)S(1)}, u32[]{:S(2)}, u32[]{:S(2)}) collective-permute-start(f32[128,256]{1,0:T(8,128)S(1)} %get-tuple-element.35), channel_id=1, source_target_pairs={{0,32},{1,5},{2,34},{3,7},{4,36},{5,1},{6,38},{7,3},{16,48},{17,21... | collective-permute-start | bytes 393224 | tf_op jit(solution)/shard_map/ppermute | solution.py:244
  201.1 5.4 %collective-permute-done.21 = f32[128,256]{1,0:T(8,128)S(1)} collective-permute-done((f32[128,256]{1,0:T(8,128)S(1)}, f32[128,256]{1,0:T(8,128)S(1)}, u32[]{:S(2)}, u32[]{:S(2)}) %collective-permute-start.21) | collective-permute-done | bytes 131104 | tf_op jit(solution)/shard_map/ppermute | solution.py:244
  206.6 1.9 collective-permute-start.33
  211.4 7.4 %collective-permute-start.23 = (f32[256,256]{1,0:T(8,128)S(1)}, f32[256,256]{1,0:T(8,128)S(1)}, u32[]{:S(2)}, u32[]{:S(2)}) collective-permute-start(f32[256,256]{1,0:T(8,128)S(1)} %fusion.4), channel_id=1, source_target_pairs={{1,0},{8,1},{17,2},{24,3},{33,4},{40,5},{49,6},{56,7},{65,8},{72,9... | collective-permute-start | bytes 786440 | tf_op jit(solution)/shard_map/ppermute | solution.py:359
  218.8 12.9 %collective-permute-start.9 = (f32[256,256]{1,0:T(8,128)S(1)}, f32[256,256]{1,0:T(8,128)S(1)}, u32[]{:S(2)}, u32[]{:S(2)}) collective-permute-start(f32[256,256]{1,0:T(8,128)S(1)} %get-tuple-element.30), channel_id=1, source_target_pairs={{9,8},{8,9},{11,10},{10,11},{13,12},{12,13},{15,14},{14,15},{25,24... | collective-permute-start | bytes 786440 | tf_op jit(solution)/shard_map/ppermute | solution.py:359
  233.0 12.4 %collective-permute-done.26.refs_5_ = f32[128,256]{1,0:T(8,128)S(1)} collective-permute-done((f32[128,256]{1,0:T(8,128)S(1)}, f32[128,256]{1,0:T(8,128)S(1)}, u32[]{:S(2)}, u32[]{:S(2)}) %collective-permute-start.26) | collective-permute-done | bytes 131104 | tf_op jit(solution)/shard_map/ppermute | solution.py:359
  247.0 2.3 shard_map.78
  (120 shorter events, 36.5 us)
Async XLA Ops:
  5.0 40.2 %all-to-all-start = ((bf16[32,32,1280]{2,1,0:T(8,128)(2,1)}), bf16[32,32,1280]{2,1,0:T(8,128)(2,1)S(1)}, u32[]{:S(2)}, u32[]{:S(2)}) async-start(bf16[32,32,1280]{2,1,0:T(8,128)(2,1)} %shard_map.73), calls=%async_computation | async-start | bytes 5242880 | tf_op jit(solution)/shard_map/all_to_all | solution.py:320
  45.2 29.1 %all-to-all-start.1 = ((bf16[32,32,768]{2,1,0:T(8,128)(2,1)}), bf16[32,32,768]{2,1,0:T(8,128)(2,1)}, u32[]{:S(2)}, u32[]{:S(2)}) async-start(bf16[32,32,768]{2,1,0:T(8,128)(2,1)} %bitcast.84), calls=%async_computation.1 | async-start | bytes 3145728 | tf_op jit(solution)/shard_map/all_to_all | solution.py:320
  54.2 52.0 %collective-permute-start = (bf16[1024,1280]{1,0:T(8,128)(2,1)S(1)}, bf16[1024,1280]{1,0:T(8,128)(2,1)}, u32[]{:S(2)}, u32[]{:S(2)}) collective-permute-start(bf16[1024,1280]{1,0:T(8,128)(2,1)S(1)} %bitcast.81), channel_id=1, source_target_pairs={{64,0},{73,1},{8,64},{1,65},{72,8},{65,9},{0,72},{9,73},{66,2},{75... | collective-permute-start | bytes 7864328 | tf_op jit(solution)/shard_map/ppermute | solution.py:334
  55.1 56.7 %collective-permute-start.14 = (bf16[1024,1280]{1,0:T(8,128)(2,1)S(1)}, bf16[1024,1280]{1,0:T(8,128)(2,1)}, u32[]{:S(2)}, u32[]{:S(2)}) collective-permute-start(bf16[1024,1280]{1,0:T(8,128)(2,1)S(1)} %bitcast.82), channel_id=1, source_target_pairs={{0,1},{1,0},{2,3},{3,2},{4,5},{5,4},{6,7},{7,6},{8,9},{9,8},{10,11... | collective-permute-start | bytes 7864328 | tf_op jit(solution)/shard_map/ppermute | solution.py:249
  74.2 34.7 %collective-permute-start.16 = (bf16[1024,768]{1,0:T(8,128)(2,1)}, bf16[1024,768]{1,0:T(8,128)(2,1)}, u32[]{:S(2)}, u32[]{:S(2)}) collective-permute-start(bf16[1024,768]{1,0:T(8,128)(2,1)} %bitcast.14), channel_id=1, source_target_pairs={{0,1},{1,0},{2,3},{3,2},{4,5},{5,4},{6,7},{7,6},{8,9},{9,8},{10,11... | collective-permute-start | bytes 4718600 | tf_op jit(solution)/shard_map/ppermute | solution.py:249
  76.2 27.9 %collective-permute-start.1 = (bf16[1024,768]{1,0:T(8,128)(2,1)}, bf16[1024,768]{1,0:T(8,128)(2,1)}, u32[]{:S(2)}, u32[]{:S(2)}) collective-permute-start(bf16[1024,768]{1,0:T(8,128)(2,1)} %bitcast.14), channel_id=1, source_target_pairs={{64,0},{73,1},{8,64},{1,65},{72,8},{65,9},{0,72},{9,73},{66,2},{75... | collective-permute-start | bytes 4718600 | tf_op jit(solution)/shard_map/ppermute | solution.py:334
  106.2 41.1 %collective-permute-start.11 = (bf16[1024,384]{1,0:T(8,128)(2,1)}, bf16[1024,384]{1,0:T(8,128)(2,1)}, u32[]{:S(2)}, u32[]{:S(2)}) collective-permute-start(bf16[1024,384]{1,0:T(8,128)(2,1)} %constant_dynamic-slice_fusion), channel_id=1, source_target_pairs={{64,0},{73,1},{8,64},{1,65},{72,8},{65,9},{0,72},{9,73},{66,2},{75... | collective-permute-start | bytes 2359304 | tf_op jit(solution)/shard_map/ppermute | solution.py:339
  108.8 25.0 %collective-permute-start.10 = (bf16[1024,640]{1,0:T(8,128)(2,1)}, bf16[1024,640]{1,0:T(8,128)(2,1)}, u32[]{:S(2)}, u32[]{:S(2)}) collective-permute-start(bf16[1024,640]{1,0:T(8,128)(2,1)} %constant_dynamic-slice_fusion.1), channel_id=1, source_target_pairs={{64,0},{73,1},{8,64},{1,65},{72,8},{65,9},{0,72},{9,73},{66,2},{75... | collective-permute-start | bytes 3932168 | tf_op jit(solution)/shard_map/ppermute | solution.py:339
  131.5 18.0 %collective-permute-start.27 = (f32[4,128,256]{2,1,0:T(8,128)}, f32[4,128,256]{2,1,0:T(8,128)S(1)}, u32[]{:S(2)}, u32[]{:S(2)}) collective-permute-start(f32[4,128,256]{2,1,0:T(8,128)} %get-tuple-element.26), channel_id=1, source_target_pairs={{0,2},{1,17},{2,4},{3,19},{4,6},{5,21},{6,0},{7,23},{16,18},{17,33... | collective-permute-start | bytes 1572872 | tf_op jit(solution)/shard_map/ppermute | solution.py:241
  133.8 19.6 %collective-permute-start.12 = (bf16[1024,640]{1,0:T(8,128)(2,1)}, bf16[1024,640]{1,0:T(8,128)(2,1)S(1)}, u32[]{:S(2)}, u32[]{:S(2)}) collective-permute-start(bf16[1024,640]{1,0:T(8,128)(2,1)} %collective-permute-done.10), channel_id=1, source_target_pairs={{0,1},{1,0},{2,3},{3,2},{4,5},{5,4},{6,7},{7,6},{8,9},{9,8},{10,11... | collective-permute-start | bytes 3932168 | tf_op jit(solution)/shard_map/ppermute | solution.py:249
  134.5 16.3 %collective-permute-start.28 = (f32[4,128,256]{2,1,0:T(8,128)}, f32[4,128,256]{2,1,0:T(8,128)}, u32[]{:S(2)}, u32[]{:S(2)}) collective-permute-start(f32[4,128,256]{2,1,0:T(8,128)} %get-tuple-element.27), channel_id=1, source_target_pairs={{0,6},{1,49},{2,0},{3,51},{4,2},{5,53},{6,4},{7,55},{16,22},{17,1}... | collective-permute-start | bytes 1572872 | tf_op jit(solution)/shard_map/ppermute | solution.py:241
  135.3 15.5 %collective-permute-start.29 = (f32[4,128,256]{2,1,0:T(8,128)}, f32[4,128,256]{2,1,0:T(8,128)}, u32[]{:S(2)}, u32[]{:S(2)}) collective-permute-start(f32[4,128,256]{2,1,0:T(8,128)} %get-tuple-element.28), channel_id=1, source_target_pairs={{0,4},{1,33},{2,6},{3,35},{4,0},{5,37},{6,2},{7,39},{16,20},{17,49... | collective-permute-start | bytes 1572872 | tf_op jit(solution)/shard_map/ppermute | solution.py:241
  147.3 26.1 %collective-permute-start.2 = (f32[4,256,256]{2,1,0:T(8,128)}, f32[4,256,256]{2,1,0:T(8,128)}, u32[]{:S(2)}, u32[]{:S(2)}) collective-permute-start(f32[4,256,256]{2,1,0:T(8,128)} %get-tuple-element.18), channel_id=1, source_target_pairs={{0,2},{1,17},{2,4},{3,19},{4,6},{5,21},{6,0},{7,23},{16,18},{17,33... | collective-permute-start | bytes 3145736 | tf_op jit(solution)/shard_map/ppermute | solution.py:241
  150.8 27.6 %collective-permute-start.3 = (f32[4,256,256]{2,1,0:T(8,128)}, f32[4,256,256]{2,1,0:T(8,128)}, u32[]{:S(2)}, u32[]{:S(2)}) collective-permute-start(f32[4,256,256]{2,1,0:T(8,128)} %get-tuple-element.19), channel_id=1, source_target_pairs={{0,6},{1,49},{2,0},{3,51},{4,2},{5,53},{6,4},{7,55},{16,22},{17,1}... | collective-permute-start | bytes 3145736 | tf_op jit(solution)/shard_map/ppermute | solution.py:241
  150.8 29.1 %collective-permute-start.4 = (f32[4,256,256]{2,1,0:T(8,128)}, f32[4,256,256]{2,1,0:T(8,128)}, u32[]{:S(2)}, u32[]{:S(2)}) collective-permute-start(f32[4,256,256]{2,1,0:T(8,128)} %get-tuple-element.20), channel_id=1, source_target_pairs={{0,4},{1,33},{2,6},{3,35},{4,0},{5,37},{6,2},{7,39},{16,20},{17,49... | collective-permute-start | bytes 3145736 | tf_op jit(solution)/shard_map/ppermute | solution.py:241
  163.0 20.8 %collective-permute-start.17 = (f32[4,128,256]{2,1,0:T(8,128)}, f32[4,128,256]{2,1,0:T(8,128)S(1)}, u32[]{:S(2)}, u32[]{:S(2)}) collective-permute-start(f32[4,128,256]{2,1,0:T(8,128)} %get-tuple-element.22), channel_id=1, source_target_pairs={{0,2},{1,17},{2,4},{3,19},{4,6},{5,21},{6,0},{7,23},{16,18},{17,33... | collective-permute-start | bytes 1572872 | tf_op jit(solution)/shard_map/ppermute | solution.py:241
  165.3 27.0 %collective-permute-start.18 = (f32[4,128,256]{2,1,0:T(8,128)}, f32[4,128,256]{2,1,0:T(8,128)S(1)}, u32[]{:S(2)}, u32[]{:S(2)}) collective-permute-start(f32[4,128,256]{2,1,0:T(8,128)} %get-tuple-element.23), channel_id=1, source_target_pairs={{0,6},{1,49},{2,0},{3,51},{4,2},{5,53},{6,4},{7,55},{16,22},{17,1}... | collective-permute-start | bytes 1572872 | tf_op jit(solution)/shard_map/ppermute | solution.py:241
  173.4 18.9 %collective-permute-start.19 = (f32[4,128,256]{2,1,0:T(8,128)}, f32[4,128,256]{2,1,0:T(8,128)S(1)}, u32[]{:S(2)}, u32[]{:S(2)}) collective-permute-start(f32[4,128,256]{2,1,0:T(8,128)} %get-tuple-element.24), channel_id=1, source_target_pairs={{0,4},{1,33},{2,6},{3,35},{4,0},{5,37},{6,2},{7,39},{16,20},{17,49... | collective-permute-start | bytes 1572872 | tf_op jit(solution)/shard_map/ppermute | solution.py:241
  178.3 17.6 %collective-permute-start.30 = (f32[128,256]{1,0:T(8,128)S(1)}, f32[128,256]{1,0:T(8,128)S(1)}, u32[]{:S(2)}, u32[]{:S(2)}) collective-permute-start(f32[128,256]{1,0:T(8,128)S(1)} %get-tuple-element.34), channel_id=1, source_target_pairs={{0,16},{1,3},{2,18},{3,5},{4,20},{5,7},{6,22},{7,1},{16,32},{17,19... | collective-permute-start | bytes 393224 | tf_op jit(solution)/shard_map/ppermute | solution.py:244
  179.9 17.6 %collective-permute-start.31 = (f32[128,256]{1,0:T(8,128)S(1)}, f32[128,256]{1,0:T(8,128)S(1)}, u32[]{:S(2)}, u32[]{:S(2)}) collective-permute-start(f32[128,256]{1,0:T(8,128)S(1)} %get-tuple-element.36), channel_id=1, source_target_pairs={{0,48},{1,7},{2,50},{3,1},{4,52},{5,3},{6,54},{7,5},{16,0},{17,23}... | collective-permute-start | bytes 393224 | tf_op jit(solution)/shard_map/ppermute | solution.py:244
  183.8 15.3 %collective-permute-start.32 = (f32[128,256]{1,0:T(8,128)S(1)}, f32[128,256]{1,0:T(8,128)S(1)}, u32[]{:S(2)}, u32[]{:S(2)}) collective-permute-start(f32[128,256]{1,0:T(8,128)S(1)} %get-tuple-element.35), channel_id=1, source_target_pairs={{0,32},{1,5},{2,34},{3,7},{4,36},{5,1},{6,38},{7,3},{16,48},{17,21... | collective-permute-start | bytes 393224 | tf_op jit(solution)/shard_map/ppermute | solution.py:244
  194.2 15.7 %collective-permute-start.5 = (f32[256,256]{1,0:T(8,128)S(1)}, f32[256,256]{1,0:T(8,128)S(1)}, u32[]{:S(2)}, u32[]{:S(2)}) collective-permute-start(f32[256,256]{1,0:T(8,128)S(1)} %get-tuple-element.31), channel_id=1, source_target_pairs={{0,16},{1,3},{2,18},{3,5},{4,20},{5,7},{6,22},{7,1},{16,32},{17,19... | collective-permute-start | bytes 786440 | tf_op jit(solution)/shard_map/ppermute | solution.py:244
  195.9 14.6 %collective-permute-start.6 = (f32[256,256]{1,0:T(8,128)S(1)}, f32[256,256]{1,0:T(8,128)S(1)}, u32[]{:S(2)}, u32[]{:S(2)}) collective-permute-start(f32[256,256]{1,0:T(8,128)S(1)} %get-tuple-element.33), channel_id=1, source_target_pairs={{0,48},{1,7},{2,50},{3,1},{4,52},{5,3},{6,54},{7,5},{16,0},{17,23}... | collective-permute-start | bytes 786440 | tf_op jit(solution)/shard_map/ppermute | solution.py:244
  197.5 13.1 %collective-permute-start.7 = (f32[256,256]{1,0:T(8,128)S(1)}, f32[256,256]{1,0:T(8,128)S(1)}, u32[]{:S(2)}, u32[]{:S(2)}) collective-permute-start(f32[256,256]{1,0:T(8,128)S(1)} %get-tuple-element.32), channel_id=1, source_target_pairs={{0,32},{1,5},{2,34},{3,7},{4,36},{5,1},{6,38},{7,3},{16,48},{17,21... | collective-permute-start | bytes 786440 | tf_op jit(solution)/shard_map/ppermute | solution.py:244
  206.6 12.2 %collective-permute-start.33 = (f32[128,256]{1,0:T(8,128)S(1)}, f32[128,256]{1,0:T(8,128)S(1)}, u32[]{:S(2)}, u32[]{:S(2)}) collective-permute-start(f32[128,256]{1,0:T(8,128)S(1)} %fusion.7), channel_id=1, source_target_pairs={{0,0},{8,1},{2,2},{10,3},{4,4},{12,5},{6,6},{14,7},{16,16},{24,17}... | collective-permute-start | bytes 393224 | tf_op jit(solution)/shard_map/ppermute | solution.py:359
  208.5 10.3 %collective-permute-start.34 = (f32[128,256]{1,0:T(8,128)S(1)}, f32[128,256]{1,0:T(8,128)S(1)}, u32[]{:S(2)}, u32[]{:S(2)}) collective-permute-start(f32[128,256]{1,0:T(8,128)S(1)} %fusion.7), channel_id=1, source_target_pairs={{1,0},{9,1},{3,2},{11,3},{5,4},{13,5},{7,6},{15,7},{17,16},{25,17}... | collective-permute-start | bytes 393224 | tf_op jit(solution)/shard_map/ppermute | solution.py:359
  209.8 21.8 %collective-permute-start.25 = (f32[128,256]{1,0:T(8,128)S(1)}, f32[128,256]{1,0:T(8,128)S(1)}, u32[]{:S(2)}, u32[]{:S(2)}) collective-permute-start(f32[128,256]{1,0:T(8,128)S(1)} %fusion.10), channel_id=1, source_target_pairs={{8,0},{9,1},{10,2},{25,3},{12,4},{41,5},{14,6},{57,7},{24,16},{11,... | collective-permute-start | bytes 393224 | tf_op jit(solution)/shard_map/ppermute | solution.py:359
  210.6 34.8 %collective-permute-start.8 = (f32[256,256]{1,0:T(8,128)S(1)}, f32[256,256]{1,0:T(8,128)S(1)}, u32[]{:S(2)}, u32[]{:S(2)}) collective-permute-start(f32[256,256]{1,0:T(8,128)S(1)} %get-tuple-element.30), channel_id=1, source_target_pairs={{0,8},{1,9},{2,10},{3,11},{4,12},{5,13},{6,14},{7,15},{16,24},{17,... | collective-permute-start | bytes 786440 | tf_op jit(solution)/shard_map/ppermute | solution.py:359
  211.4 34.0 %collective-permute-start.23 = (f32[256,256]{1,0:T(8,128)S(1)}, f32[256,256]{1,0:T(8,128)S(1)}, u32[]{:S(2)}, u32[]{:S(2)}) collective-permute-start(f32[256,256]{1,0:T(8,128)S(1)} %fusion.4), channel_id=1, source_target_pairs={{1,0},{8,1},{17,2},{24,3},{33,4},{40,5},{49,6},{56,7},{65,8},{72,9... | collective-permute-start | bytes 786440 | tf_op jit(solution)/shard_map/ppermute | solution.py:359
  218.8 26.6 %collective-permute-start.24 = (f32[256,256]{1,0:T(8,128)S(1)}, f32[256,256]{1,0:T(8,128)S(1)}, u32[]{:S(2)}, u32[]{:S(2)}) collective-permute-start(f32[256,256]{1,0:T(8,128)S(1)} %get-tuple-element.29), channel_id=1, source_target_pairs={{9,0},{0,1},{11,2},{2,3},{13,4},{4,5},{15,6},{6,7},{64,8},{73,9},{... | collective-permute-start | bytes 786440 | tf_op jit(solution)/shard_map/ppermute | solution.py:359
  218.8 26.6 %collective-permute-start.9 = (f32[256,256]{1,0:T(8,128)S(1)}, f32[256,256]{1,0:T(8,128)S(1)}, u32[]{:S(2)}, u32[]{:S(2)}) collective-permute-start(f32[256,256]{1,0:T(8,128)S(1)} %get-tuple-element.30), channel_id=1, source_target_pairs={{9,8},{8,9},{11,10},{10,11},{13,12},{12,13},{15,14},{14,15},{25,24... | collective-permute-start | bytes 786440 | tf_op jit(solution)/shard_map/ppermute | solution.py:359
  231.7 13.7 %collective-permute-start.26 = (f32[128,256]{1,0:T(8,128)S(1)}, f32[128,256]{1,0:T(8,128)S(1)}, u32[]{:S(2)}, u32[]{:S(2)}) collective-permute-start(f32[128,256]{1,0:T(8,128)S(1)} %fusion.10), channel_id=1, source_target_pairs={{0,0},{1,1},{16,2},{3,3},{32,4},{5,5},{48,6},{7,7},{2,16},{17,17},... | collective-permute-start | bytes 393224 | tf_op jit(solution)/shard_map/ppermute | solution.py:359
  (25 other events, 362.4 us)

commit v2 on v1

--- a/solution.py
+++ b/solution.py
@@ -16,6 +16,7 @@
 CHUNKS = len(PARTS)
 INTERPRET = False
 VMEM_GRANT = 60 * 2**20
+TILE_STEPS = 2
 
 
 def row_weights(row_period, row_site, period_err, site_err):
@@ -57,7 +58,7 @@
 
 def pack_first(sensitivity, row_period, row_site, period_err, site_err, depth):
     rows = sensitivity.shape[0]
-    steps = 4
+    steps = 2
     tables = [a[None, :] for a in (row_period, row_site, period_err, site_err)]
     return pl.pallas_call(
         pack_kernel,
@@ -156,7 +157,8 @@
     base = refs[2 * chunks] if based else None
     outs, scratch = refs[2 * chunks + based : 2 * chunks + based + n_out], refs[-1]
     c = pl.program_id(0)
-    height, _ = scratch.shape[2:]
+    height, tile = scratch.shape[2:]
+    columns = 4 // TILE_STEPS
     total = None
     for a, b in zip(lhs, rhs):
         part = lax.dot_general(
@@ -166,14 +168,17 @@
             preferred_element_type=jnp.float32,
         )
         total = part if total is None else total + part
-    across = lax.rem(c + 4 - scal_ref[1], 4)
-    for r in range(4):
-        down = lax.rem(r + 4 - scal_ref[0], 4)
-        s = jnp.where(scal_ref[2] == 0, down, across)
-        v = jnp.where(scal_ref[2] == 0, across, down)
-        scratch[s, v] = total[r * height : (r + 1) * height]
-
-    @pl.when(c == 3)
+    for column in range(columns):
+        across = lax.rem(c * columns + column + 4 - scal_ref[1], 4)
+        for r in range(4):
+            down = lax.rem(r + 4 - scal_ref[0], 4)
+            s = jnp.where(scal_ref[2] == 0, down, across)
+            v = jnp.where(scal_ref[2] == 0, across, down)
+            scratch[s, v] = total[
+                r * height : (r + 1) * height, column * tile : (column + 1) * tile
+            ]
+
+    @pl.when(c == TILE_STEPS - 1)
     def _():
         if n_out == 1:
             outs[0][...] = scratch[...]
@@ -203,7 +208,7 @@
         for depth in depths
     ]
     rhs_specs = [
-        pl.BlockSpec((tile, depth), lambda c, scal: (c, scal[4] if windowed else 0))
+        pl.BlockSpec((rows // TILE_STEPS, depth), lambda c, scal: (c, scal[4] if windowed else 0))
         for depth in depths
     ]
     extra = [] if base is None else [base]
@@ -218,7 +223,7 @@
         out_shape=out_shape,
         grid_spec=pltpu.PrefetchScalarGridSpec(
             num_scalar_prefetch=1,
-            grid=(4,),
+            grid=(TILE_STEPS,),
             in_specs=lhs_specs + rhs_specs + base_specs,
             out_specs=out_specs,
             scratch_shapes=[pltpu.VMEM((4, 4, height, tile), jnp.float32)],
@@ -235,14 +240,24 @@
     )(scalars, *lhs, *rhs, *extra)
 
 
-def reduce_plane(strips):
+def reduce_first(strips):
     total = strips[0]
     for shift in (1, 3, 2):
         total = total + lax.ppermute(strips[shift], PLANE, plane_shift(shift, True))
+    return total
+
+
+def reduce_second(totals):
+    heights = [total.shape[1] for total in totals]
+    total = jnp.concatenate(totals, axis=1) if len(totals) > 1 else totals[0]
     tile = total[0]
     for shift in (1, 3, 2):
         tile = tile + lax.ppermute(total[shift], PLANE, plane_shift(shift, False))
-    return tile
+    tiles, row = [], 0
+    for height in heights:
+        tiles.append(tile[row : row + height])
+        row += height
+    return tiles
 
 
 def swap_cores(value):
@@ -289,6 +304,7 @@
         cost_estimate=pl.CostEstimate(
             flops=tile * tile * 2, bytes_accessed=tile * tile * 4 * 8, transcendentals=0
         ),
+        compiler_params=pltpu.CompilerParams(vmem_limit_bytes=6 * 2**20),
         interpret=INTERPRET,
     )(scalars, *operands)
 
@@ -347,13 +363,16 @@
     strips = tile_products(
         [scaled[1], other[1]], [weighted[1], other_weighted[1]], halved, split=True, base=base
     )
-    own_tile = reduce_plane(strips)
+    own_total = reduce_first(strips)
     strips = tile_products(near, weighted, whole)
-    near_tile = reduce_plane(strips)
+    near_total = reduce_first(strips)
+    own_tile, near_tile = reduce_second([own_total, near_total])
     strips = tile_products(
         far + other_far, weighted + other_weighted, halved, split=True, windowed=True
     )
-    far_tile = reduce_plane(strips)
+    (far_tile,) = reduce_second([reduce_first(strips)])
+
+    own_tile, near_tile = lax.optimization_barrier((own_tile, near_tile))
 
     def fetch(value, place):
         return lax.ppermute(value, AXES, homes(place))

time: 250 us -> 264 us (1.056)
  the two profiles are of different devices: /device:TPU:30 before, /device:TPU:27 now
where the time goes in v2:
time: 264 us; the launch traced here: 263 us
  waiting for transfers between devices  110 us (42%)
  starting transfers between devices  76.3 us (29%)
  Pallas kernels  38.8 us (15%)
  local copies, waits for them, and re-layouts  19.8 us (8%)
  other arithmetic  17.8 us (7%)
    all_to_all x2, waiting for transfers between devices, body(): lax.all_to_all(packed, PLANE, split_axis=0, concat_axis=0, tiled=True)  49.6 us
    pallas_call x4, Pallas kernels, tile_products(): pl.pallas_call(functools.partial(tile_kernel, chunks=len(lhs), n_out=len(...  33.3 us
    ppermute x8, starting transfers between devices, fetch(): return lax.ppermute(value, AXES, homes(place))  30.5 us
    ppermute x9, waiting for transfers between devices, reduce_first(): total = total + lax.ppermute(strips[shift], PLANE, plane_shift(shift, True))  26.4 us
    all_to_all x2, starting transfers between devices, body(): lax.all_to_all(packed, PLANE, split_axis=0, concat_axis=0, tiled=True)  16.6 us
    ppermute x8, waiting for transfers between devices, fetch(): return lax.ppermute(value, AXES, homes(place))  16.3 us
    ppermute x9, starting transfers between devices, reduce_first(): total = total + lax.ppermute(strips[shift], PLANE, plane_shift(shift, True))  12.2 us
    gather x1, local copies, waits for them, and re-layouts, body(): column_var = cell_var[positions]  11.8 us
  transfers between devices with their start and end apart: 34, of which 12 were waited for; matrix products, arithmetic and copies ran while one was open for 14% of the time, Pallas kernels for 13%

profile of v2, /device:TPU:27, one launch (start us, length us, event | category | flops | bytes accessed | tf_op | source)
XLA Modules:
  0.0 262.9 jit_solution(13823128306319413655)
XLA Ops:
  0.0 3.9 %shard_map.73 = bf16[32,32,1280]{2,1,0:T(8,128)(2,1)} custom-call(s32[1,32]{1,0:T(1,128)} %bitcast.77, s32[1,32]{1,0:T(1,128)} %bitcast.75, f32[1,32]{1,0:T(1,128)} %bitcast.78, f32[1,128]{1,0:T(1,128)} %bitcast.76, f32[32,65536]{1,0:T(8,128)} %data_ref.1), custom_call_target="tpu_custom_call" | custom-call | flops 1310720 | bytes 7864320 | tf_op jit(solution)/shard_map/pallas_call | solution.py:63
  4.0 8.7 %all-to-all-start.1 = ((bf16[32,32,1280]{2,1,0:T(8,128)(2,1)}), bf16[32,32,1280]{2,1,0:T(8,128)(2,1)S(1)}, u32[]{:S(2)}, u32[]{:S(2)}) async-start(bf16[32,32,1280]{2,1,0:T(8,128)(2,1)} %shard_map.73), calls=%async_computation.1 | async-start | bytes 5242880 | tf_op jit(solution)/shard_map/all_to_all | solution.py:336
  13.1 2.1 multiply_convert_fusion.4
  16.6 29.0 %all-to-all-done.1 = bf16[32,32,1280]{2,1,0:T(8,128)(2,1)S(1)} async-done(((bf16[32,32,1280]{2,1,0:T(8,128)(2,1)}), bf16[32,32,1280]{2,1,0:T(8,128)(2,1)S(1)}, u32[]{:S(2)}, u32[]{:S(2)}) %all-to-all-start.1) | async-done | bytes 2621472 | tf_op jit(solution)/shard_map/all_to_all | solution.py:336
  45.6 7.8 %all-to-all-start = ((bf16[32,32,768]{2,1,0:T(8,128)(2,1)}), bf16[32,32,768]{2,1,0:T(8,128)(2,1)}, u32[]{:S(2)}, u32[]{:S(2)}) async-start(bf16[32,32,768]{2,1,0:T(8,128)(2,1)} %bitcast.69), calls=%async_computation | async-start | bytes 3145728 | tf_op jit(solution)/shard_map/all_to_all | solution.py:336
  54.8 20.6 %all-to-all-done = bf16[32,32,768]{2,1,0:T(8,128)(2,1)} async-done(((bf16[32,32,768]{2,1,0:T(8,128)(2,1)}), bf16[32,32,768]{2,1,0:T(8,128)(2,1)}, u32[]{:S(2)}, u32[]{:S(2)}) %all-to-all-start) | async-done | bytes 1572896 | tf_op jit(solution)/shard_map/all_to_all | solution.py:336
  78.7 11.8 %gather_fusion = f32[2048]{0:T(1024)S(1)} fusion(f32[65536]{0:T(1024)S(1)} %copy-done, s32[2048]{0:T(1024)S(1)} %broadcast_clamp_fusion), kind=kCustom, calls=%fused_computation | custom fusion | bytes 24576 | tf_op jit(solution)/shard_map/gather | solution.py:326
  92.0 2.8 %multiply_convert_fusion.3.refs_2_.refs_3_.refs_5_ = bf16[1024,768]{1,0:T(8,128)(2,1)} fusion(f32[768]{0:T(1024)S(1)} %slice.62, bf16[32,32,768]{2,1,0:T(8,128)(2,1)} %all-to-all-done), kind=kLoop, calls=%fused_computation.4 | loop fusion | flops 2359296 | bytes 3148800 | tf_op jit(solution)/shard_map/convert_element_type | solution.py:343
  94.8 6.5 %collective-permute-done.7 = bf16[1024,768]{1,0:T(8,128)(2,1)} collective-permute-done((bf16[1024,768]{1,0:T(8,128)(2,1)}, bf16[1024,768]{1,0:T(8,128)(2,1)}, u32[]{:S(2)}, u32[]{:S(2)}) %collective-permute-start.7) | collective-permute-done | bytes 1572896 | tf_op jit(solution)/shard_map/ppermute | solution.py:350
  106.2 2.2 multiply_convert_fusion.1.refs_2_.refs_4_
  108.4 2.9 %multiply_convert_fusion.2.refs_3_.refs_7_ = bf16[1024,768]{1,0:T(8,128)(2,1)} fusion(bf16[1024,768]{1,0:T(8,128)(2,1)} %collective-permute-done, f32[768]{0:T(1024)S(1)} %slice.63), kind=kLoop, calls=%fused_computation.3 | loop fusion | flops 2359296 | bytes 3148800 | tf_op jit(solution)/shard_map/convert_element_type | solution.py:343
  111.3 2.5 collective-permute-done.17
  115.9 3.7 %multiply_convert_fusion.refs_3_.refs_6_ = bf16[1024,1280]{1,0:T(8,128)(2,1)} fusion(bf16[1024,1280]{1,0:T(8,128)(2,1)} %collective-permute-done.2, f32[1280]{0:T(1024)S(1)} %bitcast.74), kind=kLoop, calls=%fused_computation.1 | loop fusion | flops 3932160 | bytes 5248000 | tf_op jit(solution)/shard_map/convert_element_type | solution.py:343
  119.7 8.2 %collective-permute-done.16 = bf16[1024,640]{1,0:T(8,128)(2,1)} collective-permute-done((bf16[1024,640]{1,0:T(8,128)(2,1)S(1)}, bf16[1024,640]{1,0:T(8,128)(2,1)}, u32[]{:S(2)}, u32[]{:S(2)}) %collective-permute-start.16) | collective-permute-done | bytes 1310752 | tf_op jit(solution)/shard_map/ppermute | solution.py:355
  127.9 2.1 collective-permute-start.18
  130.0 7.8 %shard_map.74.refs_4_ = f32[4,4,128,256]{3,2,1,0:T(8,128)} custom-call(s32[5]{0:T(128)} %stack.40.scal_ref, bf16[4,2,128,1280]{3,2,1,0:T(8,128)(2,1)} %bitcast.68, bf16[4,2,128,1280]{3,2,1,0:T(8,128)(2,1)} %bitcast.17.refs_1_, bf16[1024,1280]{1,0:T(8,128)(2,1)} %multiply_convert_fusion.1.refs_2_.refs_4_, bf16[1024,1280]{1,0:T(8,128)(2,1)} %multiply_convert_fusion.refs_3_.refs_6_), custom_call_target="tpu_custom_call" | custom-call | flops 2684354560 | bytes 9961472 | tf_op jit(solution)/shard_map/pallas_call | solution.py:219
  137.8 6.9 %shard_map.75 = (f32[4,128,256]{2,1,0:T(8,128)}, f32[4,128,256]{2,1,0:T(8,128)}, f32[4,128,256]{2,1,0:T(8,128)}, f32[4,128,256]{2,1,0:T(8,128)}) custom-call(s32[5]{0:T(128)} %stack.40.scal_ref, bf16[4,2,128,768]{3,2,1,0:T(8,128)(2,1)} %bitcast.7.refs_0_, bf16[4,2,128,768]{3,2,1,0:T(8,128)(2,1)} %bitcast.9.refs_1_, ...), custom_call_target="tpu_custom_call" | custom-call | flops 1610612736 | bytes 6815744 | tf_op jit(solution)/shard_map/pallas_call | solution.py:219
  144.7 2.8 %collective-permute-start.5 = (f32[4,128,256]{2,1,0:T(8,128)}, f32[4,128,256]{2,1,0:T(8,128)S(1)}, u32[]{:S(2)}, u32[]{:S(2)}) collective-permute-start(f32[4,128,256]{2,1,0:T(8,128)} %get-tuple-element.22), channel_id=1, source_target_pairs={{0,4},{1,33},{2,6},{3,35},{4,0},{5,37},{6,2},{7,39},{16,20},{17,49... | collective-permute-start | bytes 1572872 | tf_op jit(solution)/shard_map/ppermute | solution.py:246
  147.5 10.8 %shard_map.76 = (f32[4,256,256]{2,1,0:T(8,128)}, f32[4,256,256]{2,1,0:T(8,128)}, f32[4,256,256]{2,1,0:T(8,128)}, f32[4,256,256]{2,1,0:T(8,128)}) custom-call(s32[7]{0:T(128)} %stack.39.scal_ref, bf16[4,1,256,1280]{3,2,1,0:T(8,128)(2,1)} %bitcast.19.refs_0_, bf16[4,1,256,768]{3,2,1,0:T(8,128)(2,1)} %bitcast.21.refs_1_, ...), custom_call_target="tpu_custom_call" | custom-call | flops 4294967296 | bytes 12582912 | tf_op jit(solution)/shard_map/pallas_call | solution.py:219
  158.5 2.6 collective-permute-start.9
  161.1 2.7 %collective-permute-start.4 = (f32[4,128,256]{2,1,0:T(8,128)}, f32[4,128,256]{2,1,0:T(8,128)}, u32[]{:S(2)}, u32[]{:S(2)}) collective-permute-start(f32[4,128,256]{2,1,0:T(8,128)} %get-tuple-element.21), channel_id=1, source_target_pairs={{0,6},{1,49},{2,0},{3,51},{4,2},{5,53},{6,4},{7,55},{16,22},{17,1}... | collective-permute-start | bytes 1572872 | tf_op jit(solution)/shard_map/ppermute | solution.py:246
  164.8 7.7 %shard_map.77 = (f32[4,128,256]{2,1,0:T(8,128)}, f32[4,128,256]{2,1,0:T(8,128)}, f32[4,128,256]{2,1,0:T(8,128)}, f32[4,128,256]{2,1,0:T(8,128)}) custom-call(s32[5]{0:T(128)} %stack.40.scal_ref, bf16[4,2,128,640]{3,2,1,0:T(8,128)(2,1)} %bitcast.26.refs_0_, bf16[4,2,128,384]{3,2,1,0:T(8,128)(2,1)} %bitcast.27.refs_1_, bf16[4,2,128,640]{3,2,1,0:T(8,128)(2,1)} %bitcast.71, ...), custom_call_target="tpu_custom_call" | custom-call | flops 2147483648 | bytes 8388608 | tf_op jit(solution)/shard_map/pallas_call | solution.py:219
  172.6 16.8 %collective-permute-done.4 = f32[4,128,256]{2,1,0:T(8,128)} collective-permute-done((f32[4,128,256]{2,1,0:T(8,128)}, f32[4,128,256]{2,1,0:T(8,128)}, u32[]{:S(2)}, u32[]{:S(2)}) %collective-permute-start.4) | collective-permute-done | bytes 524320 | tf_op jit(solution)/shard_map/ppermute | solution.py:246
  189.4 2.5 collective-permute-start.22
  200.7 8.1 %collective-permute-done.21 = f32[4,128,256]{2,1,0:T(8,128)S(1)} collective-permute-done((f32[4,128,256]{2,1,0:T(8,128)}, f32[4,128,256]{2,1,0:T(8,128)S(1)}, u32[]{:S(2)}, u32[]{:S(2)}) %collective-permute-start.21) | collective-permute-done | bytes 524320 | tf_op jit(solution)/shard_map/ppermute | solution.py:246
  211.5 2.4 collective-permute-start.23
  214.3 10.3 %collective-permute-start.14 = (f32[256,256]{1,0:T(8,128)S(1)}, f32[256,256]{1,0:T(8,128)S(1)}, u32[]{:S(2)}, u32[]{:S(2)}) collective-permute-start(f32[256,256]{1,0:T(8,128)S(1)} %slice.73), channel_id=1, source_target_pairs={{0,8},{1,9},{2,10},{3,11},{4,12},{5,13},{6,14},{7,15},{16,24},{17,... | collective-permute-start | bytes 786440 | tf_op jit(solution)/shard_map/ppermute | solution.py:378
  226.5 7.1 %collective-permute-start.31 = (f32[128,256]{1,0:T(8,128)S(1)}, f32[128,256]{1,0:T(8,128)S(1)}, u32[]{:S(2)}, u32[]{:S(2)}) collective-permute-start(f32[128,256]{1,0:T(8,128)S(1)} %slice.72), channel_id=1, source_target_pairs={{1,0},{9,1},{3,2},{11,3},{5,4},{13,5},{7,6},{15,7},{17,16},{25,17}... | collective-permute-start | bytes 393224 | tf_op jit(solution)/shard_map/ppermute | solution.py:378
  233.9 4.2 %collective-permute-start.27 = (f32[256,256]{1,0:T(8,128)S(1)}, f32[256,256]{1,0:T(8,128)S(1)}, u32[]{:S(2)}, u32[]{:S(2)}) collective-permute-start(f32[256,256]{1,0:T(8,128)S(1)} %get-tuple-element.39), channel_id=1, source_target_pairs={{9,0},{0,1},{11,2},{2,3},{13,4},{4,5},{15,6},{6,7},{64,8},{73,9},{... | collective-permute-start | bytes 786440 | tf_op jit(solution)/shard_map/ppermute | solution.py:378
  238.8 6.2 %collective-permute-start.29 = (f32[128,256]{1,0:T(8,128)S(1)}, f32[128,256]{1,0:T(8,128)S(1)}, u32[]{:S(2)}, u32[]{:S(2)}) collective-permute-start(f32[128,256]{1,0:T(8,128)S(1)} %fusion.14), channel_id=1, source_target_pairs={{0,0},{1,1},{16,2},{3,3},{32,4},{5,5},{48,6},{7,7},{2,16},{17,17},... | collective-permute-start | bytes 393224 | tf_op jit(solution)/shard_map/ppermute | solution.py:378
  245.0 2.5 collective-permute-done.29.refs_5_
  247.5 12.0 %collective-permute-done.26.refs_2_ = f32[256,256]{1,0:T(8,128)S(1)} collective-permute-done((f32[256,256]{1,0:T(8,128)S(1)}, f32[256,256]{1,0:T(8,128)S(1)}, u32[]{:S(2)}, u32[]{:S(2)}) %collective-permute-start.26) | collective-permute-done | bytes 262176 | tf_op jit(solution)/shard_map/ppermute | solution.py:378
  (98 shorter events, 34.0 us)
Async XLA Ops:
  4.0 41.7 %all-to-all-start.1 = ((bf16[32,32,1280]{2,1,0:T(8,128)(2,1)}), bf16[32,32,1280]{2,1,0:T(8,128)(2,1)S(1)}, u32[]{:S(2)}, u32[]{:S(2)}) async-start(bf16[32,32,1280]{2,1,0:T(8,128)(2,1)} %shard_map.73), calls=%async_computation.1 | async-start | bytes 5242880 | tf_op jit(solution)/shard_map/all_to_all | solution.py:336
  45.6 29.7 %all-to-all-start = ((bf16[32,32,768]{2,1,0:T(8,128)(2,1)}), bf16[32,32,768]{2,1,0:T(8,128)(2,1)}, u32[]{:S(2)}, u32[]{:S(2)}) async-start(bf16[32,32,768]{2,1,0:T(8,128)(2,1)} %bitcast.69), calls=%async_computation | async-start | bytes 3145728 | tf_op jit(solution)/shard_map/all_to_all | solution.py:336
  53.5 50.3 %collective-permute-start.6 = (bf16[1024,1280]{1,0:T(8,128)(2,1)S(1)}, bf16[1024,1280]{1,0:T(8,128)(2,1)}, u32[]{:S(2)}, u32[]{:S(2)}) collective-permute-start(bf16[1024,1280]{1,0:T(8,128)(2,1)S(1)} %bitcast.66), channel_id=1, source_target_pairs={{64,0},{73,1},{8,64},{1,65},{72,8},{65,9},{0,72},{9,73},{66,2},{75... | collective-permute-start | bytes 7864328 | tf_op jit(solution)/shard_map/ppermute | solution.py:350
  75.3 26.0 %collective-permute-start.7 = (bf16[1024,768]{1,0:T(8,128)(2,1)}, bf16[1024,768]{1,0:T(8,128)(2,1)}, u32[]{:S(2)}, u32[]{:S(2)}) collective-permute-start(bf16[1024,768]{1,0:T(8,128)(2,1)} %bitcast.8), channel_id=1, source_target_pairs={{64,0},{73,1},{8,64},{1,65},{72,8},{65,9},{0,72},{9,73},{66,2},{75... | collective-permute-start | bytes 4718600 | tf_op jit(solution)/shard_map/ppermute | solution.py:350
  76.6 39.4 %collective-permute-start.2 = (bf16[1024,1280]{1,0:T(8,128)(2,1)S(1)}, bf16[1024,1280]{1,0:T(8,128)(2,1)}, u32[]{:S(2)}, u32[]{:S(2)}) collective-permute-start(bf16[1024,1280]{1,0:T(8,128)(2,1)S(1)} %bitcast.67), channel_id=1, source_target_pairs={{0,1},{1,0},{2,3},{3,2},{4,5},{5,4},{6,7},{7,6},{8,9},{9,8},{10,11... | collective-permute-start | bytes 7864328 | tf_op jit(solution)/shard_map/ppermute | solution.py:264
  78.1 30.3 %collective-permute-start = (bf16[1024,768]{1,0:T(8,128)(2,1)}, bf16[1024,768]{1,0:T(8,128)(2,1)}, u32[]{:S(2)}, u32[]{:S(2)}) collective-permute-start(bf16[1024,768]{1,0:T(8,128)(2,1)} %bitcast.8), channel_id=1, source_target_pairs={{0,1},{1,0},{2,3},{3,2},{4,5},{5,4},{6,7},{7,6},{8,9},{9,8},{10,11... | collective-permute-start | bytes 4718600 | tf_op jit(solution)/shard_map/ppermute | solution.py:264
  102.5 11.3 %collective-permute-start.17 = (bf16[1024,384]{1,0:T(8,128)(2,1)S(1)}, bf16[1024,384]{1,0:T(8,128)(2,1)}, u32[]{:S(2)}, u32[]{:S(2)}) collective-permute-start(bf16[1024,384]{1,0:T(8,128)(2,1)S(1)} %constant_dynamic-slice_fusion), channel_id=1, source_target_pairs={{64,0},{73,1},{8,64},{1,65},{72,8},{65,9},{0,72},{9,73},{66,2},{75... | collective-permute-start | bytes 2359304 | tf_op jit(solution)/shard_map/ppermute | solution.py:355
  105.2 22.6 %collective-permute-start.16 = (bf16[1024,640]{1,0:T(8,128)(2,1)S(1)}, bf16[1024,640]{1,0:T(8,128)(2,1)}, u32[]{:S(2)}, u32[]{:S(2)}) collective-permute-start(bf16[1024,640]{1,0:T(8,128)(2,1)S(1)} %constant_dynamic-slice_fusion.1), channel_id=1, source_target_pairs={{64,0},{73,1},{8,64},{1,65},{72,8},{65,9},{0,72},{9,73},{66,2},{75... | collective-permute-start | bytes 3932168 | tf_op jit(solution)/shard_map/ppermute | solution.py:355
  113.8 47.2 %collective-permute-start.19 = (bf16[1024,384]{1,0:T(8,128)(2,1)}, bf16[1024,384]{1,0:T(8,128)(2,1)}, u32[]{:S(2)}, u32[]{:S(2)}) collective-permute-start(bf16[1024,384]{1,0:T(8,128)(2,1)} %collective-permute-done.17), channel_id=1, source_target_pairs={{0,1},{1,0},{2,3},{3,2},{4,5},{5,4},{6,7},{7,6},{8,9},{9,8},{10,11... | collective-permute-start | bytes 2359304 | tf_op jit(solution)/shard_map/ppermute | solution.py:264
  127.9 35.9 %collective-permute-start.18 = (bf16[1024,640]{1,0:T(8,128)(2,1)}, bf16[1024,640]{1,0:T(8,128)(2,1)S(1)}, u32[]{:S(2)}, u32[]{:S(2)}) collective-permute-start(bf16[1024,640]{1,0:T(8,128)(2,1)} %collective-permute-done.16), channel_id=1, source_target_pairs={{0,1},{1,0},{2,3},{3,2},{4,5},{5,4},{6,7},{7,6},{8,9},{9,8},{10,11... | collective-permute-start | bytes 3932168 | tf_op jit(solution)/shard_map/ppermute | solution.py:264
  144.7 16.3 %collective-permute-start.5 = (f32[4,128,256]{2,1,0:T(8,128)}, f32[4,128,256]{2,1,0:T(8,128)S(1)}, u32[]{:S(2)}, u32[]{:S(2)}) collective-permute-start(f32[4,128,256]{2,1,0:T(8,128)} %get-tuple-element.22), channel_id=1, source_target_pairs={{0,4},{1,33},{2,6},{3,35},{4,0},{5,37},{6,2},{7,39},{16,20},{17,49... | collective-permute-start | bytes 1572872 | tf_op jit(solution)/shard_map/ppermute | solution.py:246
  158.3 34.9 %collective-permute-start.10 = (f32[4,256,256]{2,1,0:T(8,128)}, f32[4,256,256]{2,1,0:T(8,128)S(1)}, u32[]{:S(2)}, u32[]{:S(2)}) collective-permute-start(f32[4,256,256]{2,1,0:T(8,128)} %get-tuple-element.26), channel_id=1, source_target_pairs={{0,4},{1,33},{2,6},{3,35},{4,0},{5,37},{6,2},{7,39},{16,20},{17,49... | collective-permute-start | bytes 3145736 | tf_op jit(solution)/shard_map/ppermute | solution.py:246
  158.5 36.3 %collective-permute-start.9 = (f32[4,256,256]{2,1,0:T(8,128)}, f32[4,256,256]{2,1,0:T(8,128)}, u32[]{:S(2)}, u32[]{:S(2)}) collective-permute-start(f32[4,256,256]{2,1,0:T(8,128)} %get-tuple-element.25), channel_id=1, source_target_pairs={{0,6},{1,49},{2,0},{3,51},{4,2},{5,53},{6,4},{7,55},{16,22},{17,1}... | collective-permute-start | bytes 3145736 | tf_op jit(solution)/shard_map/ppermute | solution.py:246
  161.0 33.7 %collective-permute-start.8 = (f32[4,256,256]{2,1,0:T(8,128)}, f32[4,256,256]{2,1,0:T(8,128)}, u32[]{:S(2)}, u32[]{:S(2)}) collective-permute-start(f32[4,256,256]{2,1,0:T(8,128)} %get-tuple-element.24), channel_id=1, source_target_pairs={{0,2},{1,17},{2,4},{3,19},{4,6},{5,21},{6,0},{7,23},{16,18},{17,33... | collective-permute-start | bytes 3145736 | tf_op jit(solution)/shard_map/ppermute | solution.py:246
  161.1 28.4 %collective-permute-start.4 = (f32[4,128,256]{2,1,0:T(8,128)}, f32[4,128,256]{2,1,0:T(8,128)}, u32[]{:S(2)}, u32[]{:S(2)}) collective-permute-start(f32[4,128,256]{2,1,0:T(8,128)} %get-tuple-element.21), channel_id=1, source_target_pairs={{0,6},{1,49},{2,0},{3,51},{4,2},{5,53},{6,4},{7,55},{16,22},{17,1}... | collective-permute-start | bytes 1572872 | tf_op jit(solution)/shard_map/ppermute | solution.py:246
  163.7 28.2 %collective-permute-start.3 = (f32[4,128,256]{2,1,0:T(8,128)}, f32[4,128,256]{2,1,0:T(8,128)}, u32[]{:S(2)}, u32[]{:S(2)}) collective-permute-start(f32[4,128,256]{2,1,0:T(8,128)} %get-tuple-element.20), channel_id=1, source_target_pairs={{0,2},{1,17},{2,4},{3,19},{4,6},{5,21},{6,0},{7,23},{16,18},{17,33... | collective-permute-start | bytes 1572872 | tf_op jit(solution)/shard_map/ppermute | solution.py:246
  189.4 10.1 %collective-permute-start.22 = (f32[4,128,256]{2,1,0:T(8,128)}, f32[4,128,256]{2,1,0:T(8,128)S(1)}, u32[]{:S(2)}, u32[]{:S(2)}) collective-permute-start(f32[4,128,256]{2,1,0:T(8,128)} %get-tuple-element.31), channel_id=1, source_target_pairs={{0,4},{1,33},{2,6},{3,35},{4,0},{5,37},{6,2},{7,39},{16,20},{17,49... | collective-permute-start | bytes 1572872 | tf_op jit(solution)/shard_map/ppermute | solution.py:246
  191.9 16.8 %collective-permute-start.21 = (f32[4,128,256]{2,1,0:T(8,128)}, f32[4,128,256]{2,1,0:T(8,128)S(1)}, u32[]{:S(2)}, u32[]{:S(2)}) collective-permute-start(f32[4,128,256]{2,1,0:T(8,128)} %get-tuple-element.30), channel_id=1, source_target_pairs={{0,6},{1,49},{2,0},{3,51},{4,2},{5,53},{6,4},{7,55},{16,22},{17,1}... | collective-permute-start | bytes 1572872 | tf_op jit(solution)/shard_map/ppermute | solution.py:246
  193.2 15.5 %collective-permute-start.20 = (f32[4,128,256]{2,1,0:T(8,128)}, f32[4,128,256]{2,1,0:T(8,128)S(1)}, u32[]{:S(2)}, u32[]{:S(2)}) collective-permute-start(f32[4,128,256]{2,1,0:T(8,128)} %get-tuple-element.29), channel_id=1, source_target_pairs={{0,2},{1,17},{2,4},{3,19},{4,6},{5,21},{6,0},{7,23},{16,18},{17,33... | collective-permute-start | bytes 1572872 | tf_op jit(solution)/shard_map/ppermute | solution.py:246
  196.7 14.8 %collective-permute-start.13 = (f32[384,256]{1,0:T(8,128)S(1)}, f32[384,256]{1,0:T(8,128)S(1)}, u32[]{:S(2)}, u32[]{:S(2)}) collective-permute-start(f32[384,256]{1,0:T(8,128)S(1)} %get-tuple-element.34), channel_id=1, source_target_pairs={{0,32},{1,5},{2,34},{3,7},{4,36},{5,1},{6,38},{7,3},{16,48},{17,21... | collective-permute-start | bytes 1179656 | tf_op jit(solution)/shard_map/ppermute | solution.py:255
  198.0 16.1 %collective-permute-start.12 = (f32[384,256]{1,0:T(8,128)S(1)}, f32[384,256]{1,0:T(8,128)S(1)}, u32[]{:S(2)}, u32[]{:S(2)}) collective-permute-start(f32[384,256]{1,0:T(8,128)S(1)} %get-tuple-element.35), channel_id=1, source_target_pairs={{0,48},{1,7},{2,50},{3,1},{4,52},{5,3},{6,54},{7,5},{16,0},{17,23}... | collective-permute-start | bytes 1179656 | tf_op jit(solution)/shard_map/ppermute | solution.py:255
  199.5 14.6 %collective-permute-start.11 = (f32[384,256]{1,0:T(8,128)S(1)}, f32[384,256]{1,0:T(8,128)S(1)}, u32[]{:S(2)}, u32[]{:S(2)}) collective-permute-start(f32[384,256]{1,0:T(8,128)S(1)} %get-tuple-element.33), channel_id=1, source_target_pairs={{0,16},{1,3},{2,18},{3,5},{4,20},{5,7},{6,22},{7,1},{16,32},{17,19... | collective-permute-start | bytes 1179656 | tf_op jit(solution)/shard_map/ppermute | solution.py:255
  208.9 16.9 %collective-permute-start.25 = (f32[128,256]{1,0:T(8,128)S(1)}, f32[128,256]{1,0:T(8,128)S(1)}, u32[]{:S(2)}, u32[]{:S(2)}) collective-permute-start(f32[128,256]{1,0:T(8,128)S(1)} %get-tuple-element.37), channel_id=1, source_target_pairs={{0,32},{1,5},{2,34},{3,7},{4,36},{5,1},{6,38},{7,3},{16,48},{17,21... | collective-permute-start | bytes 393224 | tf_op jit(solution)/shard_map/ppermute | solution.py:255
  211.0 15.5 %collective-permute-start.24 = (f32[128,256]{1,0:T(8,128)S(1)}, f32[128,256]{1,0:T(8,128)S(1)}, u32[]{:S(2)}, u32[]{:S(2)}) collective-permute-start(f32[128,256]{1,0:T(8,128)S(1)} %get-tuple-element.38), channel_id=1, source_target_pairs={{0,48},{1,7},{2,50},{3,1},{4,52},{5,3},{6,54},{7,5},{16,0},{17,23}... | collective-permute-start | bytes 393224 | tf_op jit(solution)/shard_map/ppermute | solution.py:255
  211.5 22.2 %collective-permute-start.23 = (f32[128,256]{1,0:T(8,128)S(1)}, f32[128,256]{1,0:T(8,128)S(1)}, u32[]{:S(2)}, u32[]{:S(2)}) collective-permute-start(f32[128,256]{1,0:T(8,128)S(1)} %get-tuple-element.36), channel_id=1, source_target_pairs={{0,16},{1,3},{2,18},{3,5},{4,20},{5,7},{6,22},{7,1},{16,32},{17,19... | collective-permute-start | bytes 393224 | tf_op jit(solution)/shard_map/ppermute | solution.py:255
  214.3 24.5 %collective-permute-start.14 = (f32[256,256]{1,0:T(8,128)S(1)}, f32[256,256]{1,0:T(8,128)S(1)}, u32[]{:S(2)}, u32[]{:S(2)}) collective-permute-start(f32[256,256]{1,0:T(8,128)S(1)} %slice.73), channel_id=1, source_target_pairs={{0,8},{1,9},{2,10},{3,11},{4,12},{5,13},{6,14},{7,15},{16,24},{17,... | collective-permute-start | bytes 786440 | tf_op jit(solution)/shard_map/ppermute | solution.py:378
  224.5 20.4 %collective-permute-start.15 = (f32[256,256]{1,0:T(8,128)S(1)}, f32[256,256]{1,0:T(8,128)S(1)}, u32[]{:S(2)}, u32[]{:S(2)}) collective-permute-start(f32[256,256]{1,0:T(8,128)S(1)} %slice.73), channel_id=1, source_target_pairs={{9,8},{8,9},{11,10},{10,11},{13,12},{12,13},{15,14},{14,15},{25,24... | collective-permute-start | bytes 786440 | tf_op jit(solution)/shard_map/ppermute | solution.py:378
  225.9 8.0 %collective-permute-start.30 = (f32[128,256]{1,0:T(8,128)S(1)}, f32[128,256]{1,0:T(8,128)S(1)}, u32[]{:S(2)}, u32[]{:S(2)}) collective-permute-start(f32[128,256]{1,0:T(8,128)S(1)} %slice.72), channel_id=1, source_target_pairs={{0,0},{8,1},{2,2},{10,3},{4,4},{12,5},{6,6},{14,7},{16,16},{24,17}... | collective-permute-start | bytes 393224 | tf_op jit(solution)/shard_map/ppermute | solution.py:378
  226.5 11.5 %collective-permute-start.31 = (f32[128,256]{1,0:T(8,128)S(1)}, f32[128,256]{1,0:T(8,128)S(1)}, u32[]{:S(2)}, u32[]{:S(2)}) collective-permute-start(f32[128,256]{1,0:T(8,128)S(1)} %slice.72), channel_id=1, source_target_pairs={{1,0},{9,1},{3,2},{11,3},{5,4},{13,5},{7,6},{15,7},{17,16},{25,17}... | collective-permute-start | bytes 393224 | tf_op jit(solution)/shard_map/ppermute | solution.py:378
  233.8 25.7 %collective-permute-start.26 = (f32[256,256]{1,0:T(8,128)S(1)}, f32[256,256]{1,0:T(8,128)S(1)}, u32[]{:S(2)}, u32[]{:S(2)}) collective-permute-start(f32[256,256]{1,0:T(8,128)S(1)} %get-tuple-element.40), channel_id=1, source_target_pairs={{1,0},{8,1},{17,2},{24,3},{33,4},{40,5},{49,6},{56,7},{65,8},{72,9... | collective-permute-start | bytes 786440 | tf_op jit(solution)/shard_map/ppermute | solution.py:378
  233.9 27.4 %collective-permute-start.27 = (f32[256,256]{1,0:T(8,128)S(1)}, f32[256,256]{1,0:T(8,128)S(1)}, u32[]{:S(2)}, u32[]{:S(2)}) collective-permute-start(f32[256,256]{1,0:T(8,128)S(1)} %get-tuple-element.39), channel_id=1, source_target_pairs={{9,0},{0,1},{11,2},{2,3},{13,4},{4,5},{15,6},{6,7},{64,8},{73,9},{... | collective-permute-start | bytes 786440 | tf_op jit(solution)/shard_map/ppermute | solution.py:378
  238.8 8.8 %collective-permute-start.29 = (f32[128,256]{1,0:T(8,128)S(1)}, f32[128,256]{1,0:T(8,128)S(1)}, u32[]{:S(2)}, u32[]{:S(2)}) collective-permute-start(f32[128,256]{1,0:T(8,128)S(1)} %fusion.14), channel_id=1, source_target_pairs={{0,0},{1,1},{16,2},{3,3},{32,4},{5,5},{48,6},{7,7},{2,16},{17,17},... | collective-permute-start | bytes 393224 | tf_op jit(solution)/shard_map/ppermute | solution.py:378
  (14 other events, 345.6 us)
